TPU v7x, 32 devices: a whole 2x2x4 slice. The times are simulated.
32 devices in a mesh: group: 4 (over y, x), dev: 8 (over z, core).
Axes of the slice: x: 2, y: 2, z: 4, core: 2. Of those that a mesh axis runs over, the one named last changes fastest.
Arguments:
- q_compressed: bfloat16 [32, 1536], P('group'), may hold values from -6 to 6
- w_q_nope: bfloat16 [1536, 16384], P(None, 'dev'), may hold values from -0.15625 to 0.15625
- w_q_rope: bfloat16 [1536, 8192], P(None, 'dev'), may hold values from -0.15625 to 0.15625
- w_uk: bfloat16 [128, 128, 512], P('dev'), may hold values from -0.5 to 0.5
- w_uv: bfloat16 [128, 512, 128], P('dev'), may hold values from -0.25 to 0.25
- w_o: bfloat16 [16384, 7168], P('dev'), may hold values from -0.046875 to 0.046875
- kv_cache: bfloat16 [4, 8, 2, 2048, 576], P('group', 'dev'), may hold values from -320 to 320
- draft_kv: bfloat16 [32, 576], P('group'), may hold values from -18 to 18
- context_length: int32 [8], replicated, may hold values from 6145 to 24576
- slot_sequence: int32 [4, 8, 2], replicated, may hold values from -1 to 7, as said below
- slot_slab: int32 [4, 8, 2], replicated, may hold values from -1 to 11
Outputs:
- attn_output: float32 [32, 7168], P(('group', 'dev'))
Inputs may be any that keep to these rules, and one draw needn't show every extreme that they name: For each sequence s, slabs 0 to ceil(context_length[s] / 2048) - 1 each stand in exactly one slot of the pool, slot_sequence naming s and slot_slab the slab's number; all other slots hold -1 in both tables. The sequences' slab counts are, in some order, 4 + floor(i * 8 / 7) for i from 0 to 7. A group's slots take the slabs of its own sequences first; slabs beyond a group's 8 * 2 slots stand in free slots of other groups.
All inputs are finite; a program needn't handle non-finite values.
Results may differ from a plain program's by a relative error of at most 0.02.
The roundings to bfloat16 on the way count: a program that leaves them out, or rounds other values in their place, can miss the bound.
Values may be sent and summed in bfloat16 or wider, within the bound.
A program may use at most 128 MiB of HBM per device.

v0:
```python
import jax
import jax.numpy as jnp
from jax import lax
from jax.experimental import pallas as pl
from jax.experimental.pallas import tpu as pltpu
from jax.sharding import PartitionSpec as P

NOPE = 128
ROPE = 64
LATENT = 512
VDIM = 128
DRAFT = 4


EMPTY = -1e30


def exchange(axis, call_id, *blocks):
    count = lax.axis_size(axis)
    number = len(blocks)

    def body(*refs):
        sent, got = refs[:number], refs[number : 2 * number]
        send_sems, recv_sems, local_sems = refs[2 * number :]
        me = lax.axis_index(axis)
        barrier = pltpu.get_barrier_semaphore()
        for step in range(1, count):
            pl.semaphore_signal(
                barrier,
                inc=1,
                device_id={axis: lax.rem(me + step, count)},
                device_id_type=pl.DeviceIdType.MESH,
            )
        pl.semaphore_wait(barrier, count - 1)
        started = []
        for step in range(1, count):
            peer = lax.rem(me + step, count)
            for which in range(number):
                copy = pltpu.make_async_remote_copy(
                    src_ref=sent[which].at[peer],
                    dst_ref=got[which].at[me],
                    send_sem=send_sems.at[which, step],
                    recv_sem=recv_sems.at[which, step],
                    device_id={axis: peer},
                    device_id_type=pl.DeviceIdType.MESH,
                )
                copy.start()
                started.append(copy)
        own = []
        for which in range(number):
            copy = pltpu.make_async_copy(
                sent[which].at[me], got[which].at[me], local_sems.at[which]
            )
            copy.start()
            own.append(copy)
        for copy in own:
            copy.wait()
        for copy in started:
            copy.wait()

    vmem = pl.BlockSpec(memory_space=pltpu.VMEM)
    return pl.pallas_call(
        body,
        out_shape=tuple(jax.ShapeDtypeStruct(block.shape, block.dtype) for block in blocks),
        in_specs=[vmem] * number,
        out_specs=tuple([vmem] * number),
        scratch_shapes=[
            pltpu.SemaphoreType.DMA((number, count)),
            pltpu.SemaphoreType.DMA((number, count)),
            pltpu.SemaphoreType.DMA((number,)),
        ],
        compiler_params=pltpu.CompilerParams(
            collective_id=call_id, has_side_effects=True, vmem_limit_bytes=8 * 1024 * 1024
        ),
        name="exchange_%d" % call_id,
    )(*blocks)


def exchange_partials(axis, call_id, block_log, block_mix):
    count = lax.axis_size(axis)
    flat_log = block_log.reshape(count, 1, -1)
    width = flat_log.shape[2]
    padded = -(-width // 128) * 128
    flat_log = jnp.pad(flat_log, ((0, 0), (0, 0), (0, padded - width)))
    flat_mix = block_mix.astype(jnp.bfloat16).reshape(count, -1, block_mix.shape[-1])
    got_log, got_mix = exchange(axis, call_id, flat_log, flat_mix)
    return (
        got_log[:, :, :width].reshape(block_log.shape),
        got_mix.reshape(block_mix.shape).astype(jnp.float32),
    )


def attend_slots(call_id, every_seq, cache_slots, context_length, slot_sequence, slot_slab):
    count = lax.axis_size("dev")
    slot_count, key_width, slab_length = cache_slots.shape
    seq_total, rows, _ = every_seq.shape
    chunk = min(count, max(1, 128 // rows))
    while count % chunk:
        chunk -= 1
    steps = count // chunk
    lanes = -(-rows // 128) * 128
    log_rows = -(-slot_count // 8) * 8

    def body(
        lengths, owners, slabs, every, cache, got_log, got_mix,
        staged, arrived, keys, log_stage, mix_stage,
        key_sems, send_sems, arrive_sems, back_send, back_recv,
    ):
        group = lax.axis_index("group")
        me = lax.axis_index("dev")
        barrier = pltpu.get_barrier_semaphore()

        def greet(step, carry):
            pl.semaphore_signal(
                barrier,
                inc=1,
                device_id={"dev": lax.rem(me + step, count)},
                device_id_type=pl.DeviceIdType.MESH,
            )
            return carry

        lax.fori_loop(1, count, greet, 0)
        for slot in range(slot_count):
            pltpu.make_async_copy(cache.at[slot], keys.at[slot], key_sems.at[slot]).start()
        pl.semaphore_wait(barrier, count - 1)

        def row_copy(peer, source):
            return pltpu.make_async_remote_copy(
                src_ref=staged.at[peer],
                dst_ref=arrived.at[source],
                send_sem=send_sems.at[peer],
                recv_sem=arrive_sems.at[source],
                device_id={"dev": peer},
                device_id_type=pl.DeviceIdType.MESH,
            )

        def back_copies(peer, source):
            return [
                pltpu.make_async_remote_copy(
                    src_ref=stage.at[peer],
                    dst_ref=target.at[source],
                    send_sem=back_send.at[which, peer],
                    recv_sem=back_recv.at[which, source],
                    device_id={"dev": peer},
                    device_id_type=pl.DeviceIdType.MESH,
                )
                for which, (stage, target) in enumerate([(log_stage, got_log), (mix_stage, got_mix)])
            ]

        def send_rows(step, carry):
            peer = lax.rem(me + step, count)
            for slot in range(slot_count):
                owner = jnp.maximum(owners[group, peer, slot], 0)
                staged[peer, slot] = every[owner]
            row_copy(peer, me).start()
            return carry

        lax.fori_loop(1, count, send_rows, 0)
        limits = []
        for slot in range(slot_count):
            owner = owners[group, me, slot]
            arrived[me, slot] = every[jnp.maximum(owner, 0)]
            left = lengths[jnp.maximum(owner, 0)] - slabs[group, me, slot] * slab_length
            limits.append(jnp.where(owner >= 0, left, 0))
        for slot in range(slot_count):
            pltpu.make_async_copy(cache.at[slot], keys.at[slot], key_sems.at[slot]).wait()

        def one_step(step, carry):
            first = lax.rem(me // chunk + steps - step, steps) * chunk
            for at in range(chunk):
                source = first + at

                @pl.when(source != me)
                def _():
                    row_copy(source, source).wait_recv()

            for slot in range(slot_count):
                block = arrived[pl.ds(first, chunk), slot].reshape(chunk * rows, key_width)
                scores = lax.dot_general(
                    block, keys[slot], (((1,), (0,)), ((), ())), preferred_element_type=jnp.float32
                )
                place = lax.broadcasted_iota(jnp.int32, (1, slab_length), 1)
                is_valid = place < limits[slot]
                masked = jnp.where(is_valid, scores, EMPTY)
                peak = jnp.max(masked, axis=1, keepdims=True)
                weights = jnp.where(is_valid, jnp.exp(masked - peak), 0.0)
                total = jnp.maximum(jnp.sum(weights, axis=1, keepdims=True), 1.0)
                mixture = lax.dot_general(
                    weights.astype(jnp.bfloat16),
                    keys[slot, :LATENT],
                    (((1,), (1,)), ((), ())),
                    preferred_element_type=jnp.float32,
                )
                log = jnp.broadcast_to(peak + jnp.log(total), (chunk * rows, 128))
                mix = (mixture / total).astype(jnp.bfloat16).reshape(chunk, rows, LATENT)
                for at in range(chunk):
                    mix_stage[first + at, slot] = mix[at]
                    turned = jnp.transpose(log[at * rows : (at + 1) * rows])
                    log_stage[first + at, slot : slot + 1, :rows] = turned[:1]
            for at in range(chunk):
                source = first + at

                @pl.when(source != me)
                def _():
                    for copy in back_copies(source, me):
                        copy.start()

            return carry

        lax.fori_loop(0, steps, one_step, 0)
        got_log[me] = log_stage[me]
        got_mix[me] = mix_stage[me]

        def finish(step, carry):
            peer = lax.rem(me + step, count)
            row_copy(peer, peer).wait_send()
            for copy in back_copies(peer, peer):
                copy.wait_send()
                copy.wait_recv()
            return carry

        lax.fori_loop(1, count, finish, 0)

    smem = pl.BlockSpec(memory_space=pltpu.SMEM)
    vmem = pl.BlockSpec(memory_space=pltpu.VMEM)
    log_shape = (count, log_rows, lanes)
    mix_shape = (count, slot_count, rows, LATENT)
    got_log, got_mix = pl.pallas_call(
        body,
        out_shape=(
            jax.ShapeDtypeStruct(log_shape, jnp.float32),
            jax.ShapeDtypeStruct(mix_shape, jnp.bfloat16),
        ),
        in_specs=[smem, smem, smem, vmem, pl.BlockSpec(memory_space=pl.ANY)],
        out_specs=(vmem, vmem),
        scratch_shapes=[
            pltpu.VMEM((count, slot_count, rows, key_width), jnp.bfloat16),
            pltpu.VMEM((count, slot_count, rows, key_width), jnp.bfloat16),
            pltpu.VMEM((slot_count, key_width, slab_length), jnp.bfloat16),
            pltpu.VMEM(log_shape, jnp.float32),
            pltpu.VMEM(mix_shape, jnp.bfloat16),
            pltpu.SemaphoreType.DMA((slot_count,)),
            pltpu.SemaphoreType.DMA((count,)),
            pltpu.SemaphoreType.DMA((count,)),
            pltpu.SemaphoreType.DMA((2, count)),
            pltpu.SemaphoreType.DMA((2, count)),
        ],
        compiler_params=pltpu.CompilerParams(
            collective_id=call_id, has_side_effects=True, vmem_limit_bytes=24 * 1024 * 1024
        ),
        name="attend_slots",
    )(
        context_length,
        slot_sequence,
        slot_slab,
        every_seq,
        cache_slots,
    )
    return got_log[:, :slot_count, :rows], got_mix.astype(jnp.float32)


def merge_blocks(block_log, block_out, block_owner, own_log, own_out):
    owners_count = own_log.shape[0]
    matches = block_owner[None, :] == jnp.arange(owners_count, dtype=jnp.int32)[:, None]
    picked = jnp.where(matches[:, :, None, None], block_log[None], EMPTY)
    top_log = jnp.maximum(jnp.max(picked, axis=1), own_log)
    weights = jnp.where(matches[:, :, None, None], jnp.exp(picked - top_log[:, None]), 0.0)
    own_weight = jnp.exp(own_log - top_log)
    weight_sum = jnp.sum(weights, axis=1) + own_weight
    summed = jnp.einsum("sbtx,btxl->stxl", weights, block_out, precision=lax.Precision.HIGHEST)
    summed = summed + own_weight[..., None] * own_out
    return (top_log + jnp.log(weight_sum), summed / weight_sum[..., None])


def draft_partials(queries_seq, draft_rows):
    scores = jnp.einsum(
        "sthk,suk->sthu", queries_seq, draft_rows, preferred_element_type=jnp.float32
    )
    causal = jnp.arange(DRAFT)[None, :] <= jnp.arange(DRAFT)[:, None]
    masked = jnp.where(causal[None, :, None, :], scores, EMPTY)
    draft_peak = jnp.max(masked, axis=3)
    weights = jnp.where(causal[None, :, None, :], jnp.exp(masked - draft_peak[..., None]), 0.0)
    draft_total = jnp.sum(weights, axis=3)
    mixture = jnp.einsum(
        "sthu,sul->sthl",
        weights.astype(jnp.bfloat16),
        draft_rows[..., :LATENT],
        preferred_element_type=jnp.float32,
    )
    return (draft_peak + jnp.log(draft_total), mixture / draft_total[..., None])


def shards(
    q_compressed,
    w_q_nope,
    w_q_rope,
    w_uk,
    w_uv,
    w_o,
    kv_cache,
    draft_kv,
    context_length,
    slot_sequence,
    slot_slab,
):
    group_count = lax.axis_size("group")
    holder_count = lax.axis_size("dev")
    group_index = lax.axis_index("group")
    token_count = q_compressed.shape[0]
    seq_group = token_count // DRAFT
    heads_here = w_uk.shape[0]
    key_width = LATENT + ROPE
    q_nope = jnp.dot(q_compressed, w_q_nope, preferred_element_type=jnp.float32).astype(
        jnp.bfloat16
    )
    q_nope = q_nope.reshape(token_count, heads_here, NOPE)
    q_rope = jnp.dot(q_compressed, w_q_rope, preferred_element_type=jnp.float32).reshape(
        token_count, heads_here, ROPE
    )
    absorbed = jnp.einsum("thn,hnl->thl", q_nope, w_uk, preferred_element_type=jnp.float32)
    queries = (jnp.concatenate([absorbed, q_rope], axis=2) * (NOPE + ROPE) ** (-0.5)).astype(
        jnp.bfloat16
    )
    queries_seq = queries.reshape(seq_group, DRAFT, heads_here, key_width)
    draft_log, draft_mix = draft_partials(
        queries_seq, draft_kv.reshape(seq_group, DRAFT, key_width)
    )
    group_table = lax.dynamic_index_in_dim(slot_sequence, group_index, 0, keepdims=False)
    outgoing = jnp.broadcast_to(
        queries_seq.reshape(1, -1, key_width), (group_count, token_count * heads_here, key_width)
    )
    (gathered,) = exchange("group", 0, outgoing)
    back_log, back_mix = attend_slots(
        1,
        gathered.reshape(group_count * seq_group, DRAFT * heads_here, key_width),
        jnp.swapaxes(kv_cache[0, 0], 1, 2),
        context_length,
        slot_sequence,
        slot_slab,
    )
    seq_total = group_count * seq_group
    group_log, group_mix = merge_blocks(
        back_log.reshape(-1, DRAFT, heads_here),
        back_mix.reshape(-1, DRAFT, heads_here, LATENT),
        group_table.reshape(-1),
        jnp.full((seq_total, DRAFT, heads_here), EMPTY, jnp.float32),
        jnp.zeros((seq_total, DRAFT, heads_here, LATENT), jnp.float32),
    )
    home_log, home_mix = exchange_partials(
        "group",
        3,
        group_log.reshape(group_count, seq_group, DRAFT, heads_here),
        group_mix.reshape(group_count, seq_group, DRAFT, heads_here, LATENT),
    )
    home_owner = jnp.tile(jnp.arange(seq_group, dtype=jnp.int32), group_count)
    final_log, final_mix = merge_blocks(
        home_log.reshape(-1, DRAFT, heads_here),
        home_mix.reshape(-1, DRAFT, heads_here, LATENT),
        home_owner,
        draft_log,
        draft_mix,
    )
    attended = final_mix.astype(jnp.bfloat16).reshape(token_count, heads_here, LATENT)
    head_values = jnp.einsum("thl,hlv->thv", attended, w_uv, preferred_element_type=jnp.float32)
    head_values = head_values.astype(jnp.bfloat16).reshape(token_count, heads_here * VDIM)
    partial = jnp.dot(head_values, w_o, preferred_element_type=jnp.float32)
    (terms,) = exchange(
        "dev", 4, partial.reshape(holder_count, token_count // holder_count, -1)
    )
    return jnp.sum(terms, axis=0)


def solution(mesh):
    placed = (
        P("group", None),
        P(None, "dev"),
        P(None, "dev"),
        P("dev", None, None),
        P("dev", None, None),
        P("dev", None),
        P("group", "dev", None, None, None),
        P("group", None),
        P(),
        P(),
        P(),
    )
    return jax.shard_map(
        shards, mesh=mesh, in_specs=placed, out_specs=P(("group", "dev"), None), check_vma=False
    )
```

profile of v0, /device:TPU:0, one launch (start us, length us, event | category | flops | bytes accessed | tf_op | source)
XLA Modules:
  0.0 131.7 jit_solution(4728094897366926223)
XLA Ops:
  0.0 0.6 iota_compare_fusion.1
  0.6 1.0 constant_dynamic-slice_fusion
  1.6 0.1 eq.50
  1.7 0.5 iota_compare_fusion.2
  2.2 0.1 copy.83
  2.3 0.1 eq.46
  2.3 0.6 iota_compare_fusion
  2.9 0.7 reshape.196
  3.6 0.7 reshape.192
  4.3 0.8 copy.86.slabs
  5.1 0.8 copy.85.owners
  5.9 1.3 fusion.55
  7.2 0.7 concatenate.22
  7.9 0.1 concatenate.19
  7.9 4.6 %convolution_bitcast_fusion.1 = f32[8,16,512]{2,0,1:T(8,128)S(1)} fusion(bf16[16,128,512]{2,1,0:T(8,128)(2,1)} %param.14, bf16[8,1536]{1,0:T(8,128)(2,1)S(1)} %copy-done.5, bf16[1536,2048]{1,0:T(8,128)(2,1)} %param.12), kind=kOutput, calls=%fused_computation.9 | convolution fusion | flops 67125248 | bytes 8675328 | tf_op jit(solution)/shard_map/thn,hnl->thl/dot_general | solution.py:320
  12.5 0.2 copy.84
  12.7 1.2 fusion.54
  14.0 0.8 fusion.39
  14.8 12.1 %exchange_0.1 = bf16[4,128,576]{2,1,0:T(8,128)(2,1)S(1)} custom-call(bf16[4,128,576]{2,1,0:T(8,128)(2,1)S(1)} %broadcast_in_dim.118.refs_0_), custom_call_target="tpu_custom_call" | custom-call | tf_op jit(solution)/shard_map/exchange_0/pallas_call | solution.py:62
  26.9 2.3 %copy-done.1 = bf16[1,1,2,2048,576]{3,4,2,1,0:T(8,128)(2,1)S(1)} copy-done((bf16[1,1,2,2048,576]{3,4,2,1,0:T(8,128)(2,1)S(1)}, bf16[1,1,2,2048,576]{3,4,2,1,0:T(8,128)(2,1)}, u32[]{:S(2)}) %copy-start.1) | copy-done | bytes 4718616
  29.2 60.4 %attend_slots.1 = (f32[8,8,128]{2,1,0:T(8,128)S(1)}, bf16[8,2,64,512]{3,2,1,0:T(8,128)(2,1)S(1)}) custom-call(s32[8]{0:T(128)S(1)} %copy-done.2, s32[4,8,2]{2,1,0:T(8,128)S(1)} %copy.85.owners, s32[4,8,2]{2,1,0:T(8,128)S(1)} %copy.86.slabs, bf16[8,64,576]{2,1,0:T(8,128)(2,1)S(1)} %bitcast.61, bf16[2,576,2048]{2,1,0:T(8,128)(2,1)S(1)} %bitcast.60), custom_call_target="tpu_custom_call" | custom-call | tf_op jit(solution)/shard_map/attend_slots/pallas_call | solution.py:228
  89.6 1.0 copy-done.3
  90.6 0.1 broadcast_in_dim.119
  90.7 0.1 copy.87
  90.8 0.1 select_reduce_fusion
  90.9 0.1 copy.88
  91.0 0.1 max.39
  91.1 0.3 fusion.18
  91.5 0.1 reduce_sum.41
  91.6 2.4 %fusion.2 = bf16[8,4,16,512]{3,0,2,1:T(8,128)(2,1)S(1)} fusion(bf16[16,4,16,512]{3,2,1,0:T(8,128)(2,1)} %bitcast.63, f32[8,4,16]{0,2,1:T(8,128)S(1)} %get-tuple-element.16, f32[8,4,16]{0,2,1:T(8,128)S(1)} %get-tuple-element.15, f32[8,4,16]{0,2,1:T(8,128)S(1)} %broadcast_maximum_fusion, f32[16,4,16]{0,2,1:T(8,128)S(1)} %copy.87, pred[8,16]{1,0:T(8,128)(4,1)S(1)} %copy-done.6), kind=kOutput, calls=%fused_computation.4 | convolution fusion | flops 51142656 | bytes 1583232 | tf_op jit(solution)/shard_map/sbtx,btxl->stxl/dot_general | solution.py:270
  94.0 0.2 copy.91
  94.2 10.1 %exchange_3.1 = (f32[4,1,128]{2,1,0:T(1,128)S(1)}, bf16[4,128,512]{2,1,0:T(8,128)(2,1)S(1)}) custom-call(f32[4,1,128]{2,1,0:T(1,128)S(1)} %log_add_fusion.1.refs_0_, bf16[4,128,512]{2,1,0:T(8,128)(2,1)S(1)} %bitcast.62), custom_call_target="tpu_custom_call" | custom-call | tf_op jit(solution)/shard_map/exchange_3/pallas_call | solution.py:62
  104.3 0.8 copy-done.4
  105.1 0.5 broadcast.69
  105.6 0.7 reduce.4
  106.3 0.1 broadcast_in_dim.127
  106.4 0.1 copy.92
  106.4 0.1 select_reduce_fusion.1
  106.6 0.1 copy.94
  106.7 0.1 copy.95
  106.8 2.6 %fusion.10 = f32[4,16,512,2]{2,3,1,0:T(2,128)} fusion(bf16[8,4,16,512]{3,2,1,0:T(8,128)(2,1)} %bitcast.64, pred[2,8]{1,0:T(4,128)(4,1)S(1)} %copy-done.7, f32[2,4,16]{0,2,1:T(8,128)S(1)} %copy.95, f32[8,4,16]{0,2,1:T(8,128)S(1)} %copy.92), kind=kOutput, calls=%fused_computation.16 | convolution fusion | flops 6294528 | bytes 789008 | tf_op jit(solution)/shard_map/sbtx,btxl->stxl/dot_general | solution.py:270
  109.4 0.3 fusion.30
  109.6 0.1 copy.98
  109.8 1.3 fusion.6
  111.0 12.3 %fusion.12 = f32[8,7168]{1,0:T(8,128)S(1)} fusion(bf16[2048,7168]{1,0:T(8,128)(2,1)} %param.16, bf16[16,512,128]{2,1,0:T(8,128)(2,1)} %param.15, bf16[8,16,512]{2,1,0:T(8,128)(2,1)S(1)} %bitcast.67), kind=kOutput, calls=%fused_computation.18 | convolution fusion | flops 251674624 | bytes 31817728 | tf_op jit(solution)/shard_map/dot_general | solution.py:366
  123.3 0.2 reshape.195.refs_0_
  123.5 7.4 %exchange_4.1 = f32[8,1,7168]{2,1,0:T(1,128)S(1)} custom-call(f32[8,1,7168]{2,1,0:T(1,128)S(1)} %reshape.195.refs_0_), custom_call_target="tpu_custom_call" | custom-call | tf_op jit(solution)/shard_map/exchange_4/pallas_call | solution.py:62
  130.9 0.8 reduce_sum.44
  (25 shorter events, 0.3 us)
Async XLA Ops:
  0.0 5.9 %copy-start = (bf16[1536,1024]{1,0:T(8,128)(2,1)S(1)}, bf16[1536,1024]{1,0:T(8,128)(2,1)}, u32[]{:S(2)}) copy-start(bf16[1536,1024]{1,0:T(8,128)(2,1)} %param.13) | copy-start | bytes 9437188
  0.0 7.9 %copy-start.5 = (bf16[8,1536]{1,0:T(8,128)(2,1)S(1)}, bf16[8,1536]{1,0:T(8,128)(2,1)}, u32[]{:S(2)}) copy-start(bf16[8,1536]{1,0:T(8,128)(2,1)} %param.11) | copy-start | bytes 73732
  12.5 14.3 %copy-start.2 = (s32[8]{0:T(128)S(1)}, s32[8]{0:T(128)}, u32[]{:S(2)}) copy-start(s32[8]{0:T(128)} %lengths.1) | copy-start | bytes 100
  14.8 76.0 %copy-start.6 = (pred[8,16]{1,0:T(8,128)(4,1)S(1)}, pred[8,16]{1,0:T(8,128)(4,1)}, u32[]{:S(2)}) copy-start(pred[8,16]{1,0:T(8,128)(4,1)} %iota_compare_fusion) | copy-start | bytes 388
  26.9 2.3 %copy-start.1 = (bf16[1,1,2,2048,576]{3,4,2,1,0:T(8,128)(2,1)S(1)}, bf16[1,1,2,2048,576]{3,4,2,1,0:T(8,128)(2,1)}, u32[]{:S(2)}) copy-start(bf16[1,1,2,2048,576]{3,4,2,1,0:T(8,128)(2,1)} %param.17) | copy-start | bytes 14155780
  89.6 1.0 copy-start.3
  91.6 14.8 %copy-start.7 = (pred[2,8]{1,0:T(4,128)(4,1)S(1)}, pred[2,8]{1,0:T(4,128)(4,1)}, u32[]{:S(2)}) copy-start(pred[2,8]{1,0:T(4,128)(4,1)} %iota_compare_fusion.2) | copy-start | bytes 52
  91.6 18.2 %copy-start.8 = (pred[4,4]{1,0:T(4,128)(4,1)S(1)}, pred[4,4]{1,0:T(4,128)(4,1)}, u32[]{:S(2)}) copy-start(pred[4,4]{1,0:T(4,128)(4,1)} %iota_compare_fusion.1) | copy-start | bytes 52
  104.3 0.8 copy-start.4
where the time goes:
time: 133 us; the launch traced here: 132 us
  Pallas kernels  90 us (68%)
  matrix products  25.6 us (19%)
  local copies, waits for them, and re-layouts  11.1 us (8%)
  other arithmetic  4.82 us (4%)
    pallas_call x1, Pallas kernels, attend_slots(): pl.pallas_call(body, out_shape=(jax.ShapeDtypeStruct(log_shape, jnp.float...  60.4 us
    pallas_call x3, Pallas kernels, exchange(): pl.pallas_call(body, out_shape=tuple((jax.ShapeDtypeStruct(block.shape, b...  29.6 us
    dot_general x1, matrix products, shards(): partial = jnp.dot(head_values, w_o, preferred_element_type=jnp.float32)  12.3 us
    unnamed x20, local copies, waits for them, and re-layouts  5.68 us
    dot_general x2, matrix products, merge_blocks(): jnp.einsum('sbtx,btxl->stxl', weights, block_out, precision=lax.Precision...  4.96 us
    dot_general x1, matrix products, shards(): jnp.einsum('thn,hnl->thl', q_nope, w_uk, preferred_element_type=jnp.float32)  4.6 us

commit v1 on v0

--- a/solution.py
+++ b/solution.py
@@ -290,7 +290,7 @@
     return (draft_peak + jnp.log(draft_total), mixture / draft_total[..., None])
 
 
-def shards(
+def shards_general(
     q_compressed,
     w_q_nope,
     w_q_rope,
@@ -370,6 +370,541 @@
     return jnp.sum(terms, axis=0)
 
 
+PHASES = {2: ((0, 1),), 4: ((0, 1), (2, 3))}
+CHUNKS = 4
+
+
+def flip(value, mask, extent):
+    result, bit = 0, 1
+    while bit < extent:
+        own = lax.rem(lax.div(value, bit), 2)
+        result = result + bit * (1 - own if mask & bit else own)
+        bit *= 2
+    return result
+
+
+def fused(
+    q_compressed, w_q_nope, w_q_rope, w_uk, w_uv, w_o, keys_hbm, draft_kv,
+    context_length, slot_sequence, slot_slab,
+):
+    groups, count = lax.axis_size("group"), lax.axis_size("dev")
+    planes = count // 2
+    around = groups * 2
+    phases = PHASES[planes]
+    home_tokens, q_rank = q_compressed.shape
+    tokens = groups * home_tokens
+    seqs = tokens // DRAFT
+    heads = w_uk.shape[0] // groups
+    unit = heads * DRAFT
+    rows = seqs * unit
+    slots, key_width, slab_length = keys_hbm.shape
+    width = w_o.shape[1]
+    nope_cols, rope_cols, out_rows = heads * NOPE, heads * ROPE, heads * VDIM
+    cut = width // CHUNKS
+    bf16, f32 = jnp.bfloat16, jnp.float32
+    number = len(phases)
+
+    def body(
+        lengths, owners, slabs, qc, dkv, wqn_hbm, wqr_hbm, wuk_hbm, wuv_hbm, wo_hbm, cache, out,
+        qall, dall, wqn, wqr, wuk, wuv, wo, keys, *rest,
+    ):
+        rest = list(rest)
+        take = lambda n: [rest.pop(0) for _ in range(n)]
+        zb = take(planes)
+        staged = take(planes)
+        arrived, mixs, mixg, logs, logg = (take(number) for _ in range(5))
+        zms, zmg, zls, zlg = (take(planes) for _ in range(4))
+        parts, partg, fin, fing = take(4)
+        (
+            local, g_send, g_recv, z_send, z_recv, p_send, p_recv, b_send, b_recv,
+            y_send, y_recv, r_send, r_recv, f_send, f_recv,
+        ) = rest
+        g = lax.axis_index("group")
+        d = lax.axis_index("dev")
+        z, c = lax.div(d, 2), lax.rem(d, 2)
+        me = g * 2 + c
+
+        def remote(src, dst, send, recv, to_g, to_d):
+            return pltpu.make_async_remote_copy(
+                src_ref=src, dst_ref=dst, send_sem=send, recv_sem=recv,
+                device_id=(to_g, to_d), device_id_type=pl.DeviceIdType.MESH,
+            )
+
+        def plane_peer(step):
+            return lax.rem(me + step, around)
+
+        def plane_device(j):
+            return lax.div(j, 2), z * 2 + lax.rem(j, 2)
+
+        columns = lambda size: pl.ds(pl.multiple_of(g * size, size), size)
+        loads = [
+            pltpu.make_async_copy(wqn_hbm.at[:, columns(nope_cols)], wqn, local.at[0]),
+            pltpu.make_async_copy(wqr_hbm.at[:, columns(rope_cols)], wqr, local.at[1]),
+            pltpu.make_async_copy(wuk_hbm.at[pl.ds(g * heads, heads)], wuk, local.at[2]),
+            pltpu.make_async_copy(cache, keys, local.at[3]),
+            pltpu.make_async_copy(wuv_hbm.at[pl.ds(g * heads, heads)], wuv, local.at[4]),
+            pltpu.make_async_copy(wo_hbm.at[columns(out_rows)], wo, local.at[5]),
+        ]
+        for copy in loads:
+            copy.start()
+
+        barrier = pltpu.get_barrier_semaphore()
+
+        def greet(to_g, to_d):
+            pl.semaphore_signal(
+                barrier, inc=1, device_id=(to_g, to_d), device_id_type=pl.DeviceIdType.MESH
+            )
+
+        for step in range(1, around):
+            greet(*plane_device(plane_peer(step)))
+        for step in range(1, planes):
+            for core in range(2):
+                greet(g, lax.rem(z + step, planes) * 2 + core)
+        pl.semaphore_wait(barrier, around - 1 + 2 * (planes - 1))
+
+        def group_copies(step):
+            to = lax.rem(g + step, groups)
+            return [
+                remote(qc, qall.at[g], g_send.at[0, step], g_recv.at[0, step], to, d),
+                remote(dkv, dall.at[g], g_send.at[1, step], g_recv.at[1, step], to, d),
+            ]
+
+        for step in range(1, groups):
+            for copy in group_copies(step):
+                copy.start()
+        qall[g] = qc[...]
+        dall[g] = dkv[...]
+        for step in range(1, groups):
+            for copy in group_copies(step):
+                copy.wait()
+
+        def joined(ref):
+            pieces = [ref[i].astype(f32) for i in range(groups)]
+            return jnp.concatenate(pieces, axis=0).astype(bf16)
+
+        q_tokens = joined(qall)
+        draft = joined(dall)
+        for copy in loads[:3]:
+            copy.wait()
+        nope = jnp.dot(q_tokens, wqn[...], preferred_element_type=f32).astype(bf16)
+        rope = jnp.dot(q_tokens, wqr[...], preferred_element_type=f32)
+        by_head = []
+        for h in range(heads):
+            absorbed = jnp.dot(
+                nope[:, h * NOPE : (h + 1) * NOPE], wuk[h], preferred_element_type=f32
+            )
+            pair = jnp.concatenate([absorbed, rope[:, h * ROPE : (h + 1) * ROPE]], axis=1)
+            by_head.append((pair * (NOPE + ROPE) ** (-0.5)).astype(bf16))
+        stacked = jnp.concatenate(by_head, axis=0)
+        row = lax.broadcasted_iota(jnp.int32, (rows, rows), 0)
+        col = lax.broadcasted_iota(jnp.int32, (rows, rows), 1)
+        spot = lax.rem(lax.div(row, DRAFT), heads) * tokens
+        spot = spot + lax.div(row, unit) * DRAFT + lax.rem(row, DRAFT)
+        order = jnp.where(col == spot, 1.0, 0.0).astype(bf16)
+        queries = jnp.dot(order, stacked, preferred_element_type=f32).astype(bf16)
+        zb[0][...] = queries.reshape(seqs, unit, key_width)
+
+        def z_copy(s):
+            relay = s & 1 and s > 1
+            source, over = (zb[s ^ 1], 1) if relay else (zb[0], s)
+            return remote(
+                source, zb[s], z_send.at[s], z_recv.at[s], g, flip(z, over, planes) * 2 + c
+            )
+
+        for s in range(1, planes):
+            if not (s & 1 and s > 1):
+                z_copy(s).start()
+
+        place = [(p, phases[p].index(s)) for s in range(planes) for p in range(number) if s in phases[p]]
+
+        def p_copy(s, to):
+            p, at = place[s]
+            return remote(
+                staged[s].at[to], arrived[p].at[me, :, at], p_send.at[s, to], p_recv.at[s, me],
+                *plane_device(to),
+            )
+
+        def p_arrival(s, source):
+            p, at = place[s]
+            return remote(
+                staged[s].at[source], arrived[p].at[source, :, at], p_send.at[s, source],
+                p_recv.at[s, source], *plane_device(source),
+            )
+
+        def dispatch(s):
+            p, at = place[s]
+            if s > 0:
+                z_copy(s).wait_recv()
+                if s % 2 == 0 and s + 1 < planes:
+                    z_copy(s + 1).start()
+
+            def fill(step, carry):
+                to = plane_peer(step)
+                to_g, to_d = plane_device(to)
+                for k in range(slots):
+                    staged[s][to, k] = zb[s][jnp.maximum(owners[to_g, to_d, k], 0)]
+                return carry
+
+            def send(step, carry):
+                p_copy(s, plane_peer(step)).start()
+                return carry
+
+            lax.fori_loop(1, around, fill, 0)
+            lax.fori_loop(1, around, send, 0)
+            for k in range(slots):
+                arrived[p][me, k, at] = zb[s][jnp.maximum(owners[g, d, k], 0)]
+
+        def b_copies(p, k, to, source):
+            return [
+                remote(
+                    mixs[p].at[k, to], mixg[p].at[source, k], b_send.at[p, 0, k, to],
+                    b_recv.at[p, 0, k, source], *plane_device(to),
+                ),
+                remote(
+                    logs[p].at[k, to], logg[p].at[source, k], b_send.at[p, 1, k, to],
+                    b_recv.at[p, 1, k, source], *plane_device(to),
+                ),
+            ]
+
+        def await_rows(p):
+            for s in phases[p]:
+
+                def one(step, carry):
+                    p_arrival(s, plane_peer(step)).wait_recv()
+                    return carry
+
+                lax.fori_loop(1, around, one, 0)
+
+        def attend(p, k):
+            some = len(phases[p])
+            per = some * unit
+            total_rows = around * per
+            owner = owners[g, d, k]
+            left = lengths[jnp.maximum(owner, 0)] - slabs[g, d, k] * slab_length
+            limit = jnp.where(owner >= 0, left, 0)
+            block = arrived[p][:, k].reshape(total_rows, key_width)
+            scores = lax.dot_general(
+                block, keys[k], (((1,), (0,)), ((), ())), preferred_element_type=f32
+            )
+            position = lax.broadcasted_iota(jnp.int32, (1, slab_length), 1)
+            is_valid = position < limit
+            masked = jnp.where(is_valid, scores, EMPTY)
+            peak = jnp.max(masked, axis=1, keepdims=True)
+            weights = jnp.where(is_valid, jnp.exp(masked - peak), 0.0)
+            total = jnp.maximum(jnp.sum(weights, axis=1, keepdims=True), 1.0)
+            mixture = lax.dot_general(
+                weights.astype(bf16), keys[k, :LATENT], (((1,), (1,)), ((), ())),
+                preferred_element_type=f32,
+            )
+            mixs[p][k] = (mixture / total).astype(bf16).reshape(around, some, unit, LATENT)
+            log = jnp.broadcast_to(peak + jnp.log(total), (total_rows, 128))
+            log = jnp.transpose(log)[:1]
+            for j in range(around):
+                logs[p][k, j, :, :per] = log[:, j * per : (j + 1) * per]
+
+            def send(step, carry):
+                for copy in b_copies(p, k, plane_peer(step), me):
+                    copy.start()
+                return carry
+
+            lax.fori_loop(1, around, send, 0)
+            mixg[p][me, k] = mixs[p][k, me]
+            logg[p][me, k] = logs[p][k, me]
+
+        def split_dot(weights, block):
+            high = weights.astype(bf16)
+            low = (weights - high.astype(f32)).astype(bf16)
+            return jnp.dot(high, block, preferred_element_type=f32) + jnp.dot(
+                low, block, preferred_element_type=f32
+            )
+
+        def y_copy(s):
+            to = flip(z, s, planes) * 2 + c
+            return [
+                remote(zms[s], zmg[s], y_send.at[0, s], y_recv.at[0, s], g, to),
+                remote(zls[s], zlg[s], y_send.at[1, s], y_recv.at[1, s], g, to),
+            ]
+
+        def merge_plane(p):
+            some = len(phases[p])
+            per = some * unit
+            blocks = around * slots
+
+            def one(step, carry):
+                source = plane_peer(step)
+                for k in range(slots):
+                    for copy in b_copies(p, k, source, source):
+                        copy.wait_recv()
+                return carry
+
+            lax.fori_loop(1, around, one, 0)
+            wide = blocks * per
+            cells = [logg[p][j, k, :, :per] for j in range(around) for k in range(slots)]
+            log = jnp.concatenate(cells, axis=1)
+            lane = lax.broadcasted_iota(jnp.int32, (1, wide), 1)
+            owner = jnp.full((1, wide), -1, jnp.int32)
+            for j in range(around):
+                for k in range(slots):
+                    here = owners[j // 2, z * 2 + j % 2, k]
+                    owner = jnp.where(lax.div(lane, per) == j * slots + k, here, owner)
+            tag = owner * per + lax.rem(lane, per)
+            height = some * rows
+            line = lax.broadcasted_iota(jnp.int32, (height, 1), 0)
+            inner = lax.div(line, rows) * unit + lax.rem(line, unit)
+            mark = lax.rem(lax.div(line, unit), seqs) * per + inner
+            match = tag == mark
+            picked = jnp.where(match, log, EMPTY)
+            top = jnp.max(picked, axis=1, keepdims=True)
+            weights = jnp.where(match, jnp.exp(picked - top), 0.0)
+            total = jnp.maximum(jnp.sum(weights, axis=1, keepdims=True), 1.0)
+            block = mixg[p][...].reshape(wide, LATENT)
+            mixed = (split_dot(weights, block) / total).astype(bf16)
+            logged = jnp.broadcast_to(top + jnp.log(total), (height, 128))
+            logged = jnp.transpose(logged)[:1]
+            for at, s in enumerate(phases[p]):
+                mix_to, log_to = (zms[s], zls[s]) if s > 0 else (zmg[s], zlg[s])
+                mix_to[...] = mixed[at * rows : (at + 1) * rows]
+                log_to[...] = logged[:, at * rows : (at + 1) * rows]
+            for s in phases[p]:
+                if s > 0:
+                    for copy in y_copy(s):
+                        copy.start()
+
+        def attend_slot(p):
+            def one(k, carry):
+                attend(p, k)
+                return carry
+
+            return one
+
+        for s in phases[0]:
+            dispatch(s)
+
+        scores = lax.dot_general(
+            queries, draft, (((1,), (1,)), ((), ())), preferred_element_type=f32
+        )
+        row = lax.broadcasted_iota(jnp.int32, (rows, tokens), 0)
+        col = lax.broadcasted_iota(jnp.int32, (rows, tokens), 1)
+        seen = (lax.div(row, unit) == lax.div(col, DRAFT)) & (
+            lax.rem(col, DRAFT) <= lax.rem(row, DRAFT)
+        )
+        masked = jnp.where(seen, scores, EMPTY)
+        draft_peak = jnp.max(masked, axis=1, keepdims=True)
+        weights = jnp.where(seen, jnp.exp(masked - draft_peak), 0.0)
+        draft_total = jnp.sum(weights, axis=1, keepdims=True)
+        draft_mix = jnp.dot(weights.astype(bf16), draft[:, :LATENT], preferred_element_type=f32)
+        draft_mix = draft_mix / draft_total
+        draft_log = draft_peak + jnp.log(draft_total)
+
+        loads[3].wait()
+        await_rows(0)
+        if number == 1:
+            lax.fori_loop(0, slots, attend_slot(0), 0)
+        else:
+            attend(0, 0)
+            for s in phases[1]:
+                dispatch(s)
+            lax.fori_loop(1, slots, attend_slot(0), 0)
+            await_rows(1)
+            attend(1, 0)
+            merge_plane(0)
+            lax.fori_loop(1, slots, attend_slot(1), 0)
+        merge_plane(number - 1)
+
+        for s in range(1, planes):
+            for copy in y_copy(s):
+                copy.wait_recv()
+        wide = planes * rows
+        log = jnp.concatenate([zlg[s][...] for s in range(planes)], axis=1)
+        lane = lax.broadcasted_iota(jnp.int32, (1, wide), 1)
+        line = lax.broadcasted_iota(jnp.int32, (rows, 1), 0)
+        match = lax.rem(lane, rows) == line
+        picked = jnp.where(match, log, EMPTY)
+        top = jnp.maximum(jnp.max(picked, axis=1, keepdims=True), draft_log)
+        weights = jnp.where(match, jnp.exp(picked - top), 0.0)
+        own = jnp.exp(draft_log - top)
+        total = jnp.sum(weights, axis=1, keepdims=True) + own
+        block = jnp.concatenate([zmg[s][...] for s in range(planes)], axis=0)
+        summed = split_dot(weights, block) + own * draft_mix
+        attended = (summed / total).astype(bf16)
+        row = lax.broadcasted_iota(jnp.int32, (rows, rows), 0)
+        col = lax.broadcasted_iota(jnp.int32, (rows, rows), 1)
+        token = lax.rem(row, tokens)
+        spot = lax.div(token, DRAFT) * unit + lax.div(row, tokens) * DRAFT + lax.rem(token, DRAFT)
+        order = jnp.where(col == spot, 1.0, 0.0).astype(bf16)
+        attended = jnp.dot(order, attended, preferred_element_type=f32).astype(bf16)
+        loads[4].wait()
+        loads[5].wait()
+        values = [
+            jnp.dot(attended[h * tokens : (h + 1) * tokens], wuv[h], preferred_element_type=f32)
+            for h in range(heads)
+        ]
+        values = jnp.concatenate(values, axis=1).astype(bf16)
+
+        def r_copy(n, step):
+            to = lax.rem(g + step, groups)
+            return remote(
+                parts.at[n, to], partg.at[n, g], r_send.at[n, step], r_recv.at[n, step], to, d
+            )
+
+        def project(n, carry):
+            span = pl.ds(pl.multiple_of(n * cut, 128), cut)
+            part = jnp.dot(values, wo[:, span], preferred_element_type=f32)
+            for i in range(groups):
+                parts[n, i] = part[i * home_tokens : (i + 1) * home_tokens].astype(bf16)
+            for step in range(1, groups):
+                r_copy(n, step).start()
+            partg[n, g] = parts[n, g]
+            return carry
+
+        lax.fori_loop(0, CHUNKS, project, 0)
+
+        def f_copy(n, to, source):
+            return remote(
+                fin.at[n, to], fing.at[n, source], f_send.at[n, to], f_recv.at[n, source], g, to
+            )
+
+        own_tokens = home_tokens // count
+
+        def gather(n, carry):
+            for step in range(1, groups):
+                r_copy(n, step).wait_recv()
+            summed = partg[n, 0].astype(f32)
+            for i in range(1, groups):
+                summed = summed + partg[n, i].astype(f32)
+            for t in range(count):
+                fin[n, t] = summed[t * own_tokens : (t + 1) * own_tokens]
+
+            def send(step, carry):
+                f_copy(n, lax.rem(d + step, count), d).start()
+                return carry
+
+            lax.fori_loop(1, count, send, 0)
+            fing[n, d] = fin[n, d]
+            return carry
+
+        lax.fori_loop(0, CHUNKS, gather, 0)
+
+        for n in range(CHUNKS):
+
+            def one(step, carry):
+                source = lax.rem(d + step, count)
+                f_copy(n, source, source).wait_recv()
+                return carry
+
+            lax.fori_loop(1, count, one, 0)
+            summed = fing[n, 0]
+            for t in range(1, count):
+                summed = summed + fing[n, t]
+            out[:, n * cut : (n + 1) * cut] = summed
+
+        for s in range(1, planes):
+            z_copy(s).wait_send()
+            for copy in y_copy(s):
+                copy.wait_send()
+
+        def finish(step, carry):
+            to = plane_peer(step)
+            for s in range(planes):
+                p_copy(s, to).wait_send()
+            for p in range(number):
+                for k in range(slots):
+                    for copy in b_copies(p, k, to, me):
+                        copy.wait_send()
+            return carry
+
+        lax.fori_loop(1, around, finish, 0)
+
+        def finish_chunk(n, carry):
+            for step in range(1, groups):
+                r_copy(n, step).wait_send()
+            for step in range(1, count):
+                f_copy(n, lax.rem(d + step, count), d).wait_send()
+            return carry
+
+        lax.fori_loop(0, CHUNKS, finish_chunk, 0)
+
+    smem = pl.BlockSpec(memory_space=pltpu.SMEM)
+    vmem = pl.BlockSpec(memory_space=pltpu.VMEM)
+    hbm = pl.BlockSpec(memory_space=pl.ANY)
+    own_tokens = home_tokens // count
+    scratch = [
+        pltpu.VMEM((groups, home_tokens, q_rank), bf16),
+        pltpu.VMEM((groups, home_tokens, key_width), bf16),
+        pltpu.VMEM((q_rank, nope_cols), bf16),
+        pltpu.VMEM((q_rank, rope_cols), bf16),
+        pltpu.VMEM((heads, NOPE, LATENT), bf16),
+        pltpu.VMEM((heads, LATENT, VDIM), bf16),
+        pltpu.VMEM((out_rows, width), bf16),
+        pltpu.VMEM((slots, key_width, slab_length), bf16),
+    ]
+    scratch += [pltpu.VMEM((seqs, unit, key_width), bf16) for _ in range(planes)]
+    scratch += [pltpu.VMEM((around, slots, unit, key_width), bf16) for _ in range(planes)]
+    sizes = [len(phase) for phase in phases]
+    scratch += [pltpu.VMEM((around, slots, n, unit, key_width), bf16) for n in sizes]
+    scratch += [pltpu.VMEM((slots, around, n, unit, LATENT), bf16) for n in sizes]
+    scratch += [pltpu.VMEM((around, slots, n, unit, LATENT), bf16) for n in sizes]
+    lanes = [-(-n * unit // 128) * 128 for n in sizes]
+    scratch += [pltpu.VMEM((slots, around, 1, n), f32) for n in lanes]
+    scratch += [pltpu.VMEM((around, slots, 1, n), f32) for n in lanes]
+    scratch += [pltpu.VMEM((rows, LATENT), bf16) for _ in range(2 * planes)]
+    scratch += [pltpu.VMEM((1, rows), f32) for _ in range(2 * planes)]
+    scratch += [pltpu.VMEM((CHUNKS, groups, home_tokens, cut), bf16) for _ in range(2)]
+    scratch += [pltpu.VMEM((CHUNKS, count, own_tokens, cut), f32) for _ in range(2)]
+    dma = pltpu.SemaphoreType.DMA
+    scratch += [
+        dma((6,)),
+        dma((2, groups)), dma((2, groups)),
+        dma((planes,)), dma((planes,)),
+        dma((planes, around)), dma((planes, around)),
+        dma((number, 2, slots, around)), dma((number, 2, slots, around)),
+        dma((2, planes)), dma((2, planes)),
+        dma((CHUNKS, groups)), dma((CHUNKS, groups)),
+        dma((CHUNKS, count)), dma((CHUNKS, count)),
+    ]
+    return pl.pallas_call(
+        body,
+        out_shape=jax.ShapeDtypeStruct((own_tokens, width), f32),
+        in_specs=[smem] * 3 + [vmem] * 2 + [hbm] * 6,
+        out_specs=vmem,
+        scratch_shapes=scratch,
+        compiler_params=pltpu.CompilerParams(
+            collective_id=0, has_side_effects=True, vmem_limit_bytes=56 * 1024 * 1024
+        ),
+        name="fused",
+    )(
+        context_length, slot_sequence, slot_slab, q_compressed, draft_kv,
+        w_q_nope, w_q_rope, w_uk, w_uv, w_o, keys_hbm,
+    )
+
+
+def shards(
+    q_compressed, w_q_nope, w_q_rope, w_uk, w_uv, w_o, kv_cache, draft_kv,
+    context_length, slot_sequence, slot_slab,
+):
+    args = (
+        q_compressed, w_q_nope, w_q_rope, w_uk, w_uv, w_o, kv_cache, draft_kv,
+        context_length, slot_sequence, slot_slab,
+    )
+    groups, count = lax.axis_size("group"), lax.axis_size("dev")
+    heads = w_uk.shape[0] // groups
+    fits = (
+        w_uk.shape[0] % groups == 0
+        and heads * DRAFT % 16 == 0
+        and count % 2 == 0
+        and count // 2 in PHASES
+        and q_compressed.shape[0] % count == 0
+        and w_o.shape[1] % (128 * CHUNKS) == 0
+    )
+    if not fits:
+        return shards_general(*args)
+    keys = jnp.swapaxes(kv_cache[0, 0], 1, 2)
+    return fused(
+        q_compressed, w_q_nope, w_q_rope, w_uk, w_uv, w_o, keys, draft_kv,
+        context_length, slot_sequence, slot_slab,
+    )
+
+
 def solution(mesh):
     placed = (
         P("group", None),

time: 133 us -> 82.6 us (0.62)
  matrix products: 25.6 us -> 0 us
  Pallas kernels: 90 us -> 78.1 us
  local copies, waits for them, and re-layouts: 11.1 us -> 4.12 us
  other arithmetic: 4.82 us -> 0 us
    dot_general x7 -> x0, matrix products: 25.6 us -> none  [the longest x1 12.3 us: shards(): partial = jnp.dot(head_values, w_o, preferred_element_type=jnp.float32)]
    pallas_call x4 -> x1, Pallas kernels: 90 us -> 78.1 us  [fused(): pl.pallas_call(body, out_shape=jax.ShapeDtypeStruct((own_tokens, width),...]
    reduce_sum x4 -> x0, other arithmetic: 2.08 us -> none  [the longest x1 0.79 us: shards(): return jnp.sum(terms, axis=0)]
    reshape x3 -> x0, local copies, waits for them, and re-layouts: 1.58 us -> none  [the longest x2 1.42 us: shards(): draft_kv.reshape(seq_group, DRAFT, key_width)]
    unnamed x20 -> x3, local copies, waits for them, and re-layouts: 5.68 us -> 4.12 us
where the time goes in v1:
time: 82.6 us; the launch traced here: 82.2 us
  Pallas kernels  78.1 us (95%)
  local copies, waits for them, and re-layouts  4.12 us (5%)
    pallas_call x1, Pallas kernels, fused(): pl.pallas_call(body, out_shape=jax.ShapeDtypeStruct((own_tokens, width),...  78.1 us
    unnamed x3, local copies, waits for them, and re-layouts  4.12 us

profile of v1, /device:TPU:0, one launch (start us, length us, event | category | flops | bytes accessed | tf_op | source)
XLA Modules:
  0.0 82.2 jit_solution(2253704704298278318)
XLA Ops:
  0.0 1.4 %copy.12.owners = s32[4,8,2]{2,1,0:T(8,128)} copy(s32[4,8,2]{1,2,0:T(2,128)} %param.20) | data formatting | bytes 512 | tf_op args[9]
  1.4 1.4 %copy.13.slabs = s32[4,8,2]{2,1,0:T(8,128)} copy(s32[4,8,2]{1,2,0:T(2,128)} %param.21) | data formatting | bytes 512 | tf_op args[10]
  2.8 78.1 %fused.1 = f32[1,7168]{1,0:T(1,128)} custom-call(s32[8]{0:T(128)} %lengths.1, s32[4,8,2]{2,1,0:T(8,128)} %copy.12.owners, s32[4,8,2]{2,1,0:T(8,128)} %copy.13.slabs, bf16[8,1536]{1,0:T(8,128)(2,1)} %qc.1, bf16[8,576]{1,0:T(8,128)(2,1)} %dkv.1, bf16[1536,2048]{1,0:T(8,128)(2,1)} %wqn_hbm.1, bf16[1536,1024]{1,0:T(8,128)(2,1)} %wqr_hbm.1, ...), custom_call_target="tpu_custom_call" | custom-call | tf_op jit(solution)/shard_map/fused/pallas_call | solution.py:865
  80.9 1.4 %copy.15 = f32[1,7168]{1,0:T(1,128)} copy(f32[1,7168]{1,0:T(1,128)} %fused.1) | data formatting | bytes 57344

commit v2 on v1

--- a/solution.py
+++ b/solution.py
@@ -370,7 +370,8 @@
     return jnp.sum(terms, axis=0)
 
 
-PHASES = {2: ((0, 1),), 4: ((0, 1), (2, 3))}
+PLANES = (2, 4)
+HALVES = 2
 CHUNKS = 4
 
 
@@ -390,7 +391,7 @@
     groups, count = lax.axis_size("group"), lax.axis_size("dev")
     planes = count // 2
     around = groups * 2
-    phases = PHASES[planes]
+    phases = tuple((s,) for s in range(planes))
     home_tokens, q_rank = q_compressed.shape
     tokens = groups * home_tokens
     seqs = tokens // DRAFT
@@ -414,7 +415,7 @@
         staged = take(planes)
         arrived, mixs, mixg, logs, logg = (take(number) for _ in range(5))
         zms, zmg, zls, zlg = (take(planes) for _ in range(4))
-        parts, partg, fin, fing = take(4)
+        parts, partg, fin = take(3)
         (
             local, g_send, g_recv, z_send, z_recv, p_send, p_recv, b_send, b_recv,
             y_send, y_recv, r_send, r_recv, f_send, f_recv,
@@ -437,6 +438,12 @@
             return lax.div(j, 2), z * 2 + lax.rem(j, 2)
 
         columns = lambda size: pl.ds(pl.multiple_of(g * size, size), size)
+        early = [
+            pltpu.make_async_copy(qc, qall.at[g], local.at[6]),
+            pltpu.make_async_copy(dkv, dall.at[g], local.at[7]),
+        ]
+        for copy in early:
+            copy.start()
         loads = [
             pltpu.make_async_copy(wqn_hbm.at[:, columns(nope_cols)], wqn, local.at[0]),
             pltpu.make_async_copy(wqr_hbm.at[:, columns(rope_cols)], wqr, local.at[1]),
@@ -465,15 +472,15 @@
         def group_copies(step):
             to = lax.rem(g + step, groups)
             return [
-                remote(qc, qall.at[g], g_send.at[0, step], g_recv.at[0, step], to, d),
-                remote(dkv, dall.at[g], g_send.at[1, step], g_recv.at[1, step], to, d),
+                remote(qall.at[g], qall.at[g], g_send.at[0, step], g_recv.at[0, step], to, d),
+                remote(dall.at[g], dall.at[g], g_send.at[1, step], g_recv.at[1, step], to, d),
             ]
 
+        for copy in early:
+            copy.wait()
         for step in range(1, groups):
             for copy in group_copies(step):
                 copy.start()
-        qall[g] = qc[...]
-        dall[g] = dkv[...]
         for step in range(1, groups):
             for copy in group_copies(step):
                 copy.wait()
@@ -504,16 +511,19 @@
         queries = jnp.dot(order, stacked, preferred_element_type=f32).astype(bf16)
         zb[0][...] = queries.reshape(seqs, unit, key_width)
 
-        def z_copy(s):
+        def z_copy(s, half):
             relay = s & 1 and s > 1
             source, over = (zb[s ^ 1], 1) if relay else (zb[0], s)
+            span = pl.ds(half * seqs // HALVES, seqs // HALVES)
             return remote(
-                source, zb[s], z_send.at[s], z_recv.at[s], g, flip(z, over, planes) * 2 + c
-            )
-
-        for s in range(1, planes):
-            if not (s & 1 and s > 1):
-                z_copy(s).start()
+                source.at[span], zb[s].at[span], z_send.at[s, half], z_recv.at[s, half],
+                g, flip(z, over, planes) * 2 + c,
+            )
+
+        for half in range(HALVES):
+            for s in reversed(range(1, planes)):
+                if not (s & 1 and s > 1):
+                    z_copy(s, half).start()
 
         place = [(p, phases[p].index(s)) for s in range(planes) for p in range(number) if s in phases[p]]
 
@@ -534,15 +544,16 @@
         def dispatch(s):
             p, at = place[s]
             if s > 0:
-                z_copy(s).wait_recv()
-                if s % 2 == 0 and s + 1 < planes:
-                    z_copy(s + 1).start()
+                for half in range(HALVES):
+                    z_copy(s, half).wait_recv()
+                    if s % 2 == 0 and s + 1 < planes:
+                        z_copy(s + 1, half).start()
 
             def fill(step, carry):
                 to = plane_peer(step)
                 to_g, to_d = plane_device(to)
                 for k in range(slots):
-                    staged[s][to, k] = zb[s][jnp.maximum(owners[to_g, to_d, k], 0)]
+                    staged[s][to, k] = zb[s][jnp.maximum(owners[to_g, k, to_d], 0)]
                 return carry
 
             def send(step, carry):
@@ -552,7 +563,7 @@
             lax.fori_loop(1, around, fill, 0)
             lax.fori_loop(1, around, send, 0)
             for k in range(slots):
-                arrived[p][me, k, at] = zb[s][jnp.maximum(owners[g, d, k], 0)]
+                arrived[p][me, k, at] = zb[s][jnp.maximum(owners[g, k, d], 0)]
 
         def b_copies(p, k, to, source):
             return [
@@ -579,8 +590,8 @@
             some = len(phases[p])
             per = some * unit
             total_rows = around * per
-            owner = owners[g, d, k]
-            left = lengths[jnp.maximum(owner, 0)] - slabs[g, d, k] * slab_length
+            owner = owners[g, k, d]
+            left = lengths[jnp.maximum(owner, 0)] - slabs[g, k, d] * slab_length
             limit = jnp.where(owner >= 0, left, 0)
             block = arrived[p][:, k].reshape(total_rows, key_width)
             scores = lax.dot_general(
@@ -645,7 +656,7 @@
             owner = jnp.full((1, wide), -1, jnp.int32)
             for j in range(around):
                 for k in range(slots):
-                    here = owners[j // 2, z * 2 + j % 2, k]
+                    here = owners[j // 2, k, z * 2 + j % 2]
                     owner = jnp.where(lax.div(lane, per) == j * slots + k, here, owner)
             tag = owner * per + lax.rem(lane, per)
             height = some * rows
@@ -670,16 +681,7 @@
                     for copy in y_copy(s):
                         copy.start()
 
-        def attend_slot(p):
-            def one(k, carry):
-                attend(p, k)
-                return carry
-
-            return one
-
-        for s in phases[0]:
-            dispatch(s)
-
+        dispatch(0)
         scores = lax.dot_general(
             queries, draft, (((1,), (1,)), ((), ())), preferred_element_type=f32
         )
@@ -696,19 +698,23 @@
         draft_mix = draft_mix / draft_total
         draft_log = draft_peak + jnp.log(draft_total)
 
+        def attend_both(p):
+            def one(k, carry):
+                attend(p, k)
+                return carry
+
+            await_rows(p)
+            lax.fori_loop(0, slots, one, 0)
+
         loads[3].wait()
-        await_rows(0)
-        if number == 1:
-            lax.fori_loop(0, slots, attend_slot(0), 0)
-        else:
-            attend(0, 0)
-            for s in phases[1]:
-                dispatch(s)
-            lax.fori_loop(1, slots, attend_slot(0), 0)
-            await_rows(1)
-            attend(1, 0)
-            merge_plane(0)
-            lax.fori_loop(1, slots, attend_slot(1), 0)
+        attend_both(0)
+        for s in range(1, planes):
+            dispatch(s)
+        merge_plane(0)
+        for p in range(1, number):
+            attend_both(p)
+            if p > 1:
+                merge_plane(p - 1)
         merge_plane(number - 1)
 
         for s in range(1, planes):
@@ -761,7 +767,7 @@
 
         def f_copy(n, to, source):
             return remote(
-                fin.at[n, to], fing.at[n, source], f_send.at[n, to], f_recv.at[n, source], g, to
+                fin.at[n, to], out.at[n, source], f_send.at[n, to], f_recv.at[n, source], g, to
             )
 
         own_tokens = home_tokens // count
@@ -773,14 +779,14 @@
             for i in range(1, groups):
                 summed = summed + partg[n, i].astype(f32)
             for t in range(count):
-                fin[n, t] = summed[t * own_tokens : (t + 1) * own_tokens]
+                fin[n, t] = summed[t * own_tokens : (t + 1) * own_tokens].astype(bf16)
 
             def send(step, carry):
                 f_copy(n, lax.rem(d + step, count), d).start()
                 return carry
 
             lax.fori_loop(1, count, send, 0)
-            fing[n, d] = fin[n, d]
+            out[n, d] = fin[n, d]
             return carry
 
         lax.fori_loop(0, CHUNKS, gather, 0)
@@ -793,13 +799,10 @@
                 return carry
 
             lax.fori_loop(1, count, one, 0)
-            summed = fing[n, 0]
-            for t in range(1, count):
-                summed = summed + fing[n, t]
-            out[:, n * cut : (n + 1) * cut] = summed
 
         for s in range(1, planes):
-            z_copy(s).wait_send()
+            for half in range(HALVES):
+                z_copy(s, half).wait_send()
             for copy in y_copy(s):
                 copy.wait_send()
 
@@ -850,22 +853,22 @@
     scratch += [pltpu.VMEM((rows, LATENT), bf16) for _ in range(2 * planes)]
     scratch += [pltpu.VMEM((1, rows), f32) for _ in range(2 * planes)]
     scratch += [pltpu.VMEM((CHUNKS, groups, home_tokens, cut), bf16) for _ in range(2)]
-    scratch += [pltpu.VMEM((CHUNKS, count, own_tokens, cut), f32) for _ in range(2)]
+    scratch += [pltpu.VMEM((CHUNKS, count, own_tokens, cut), bf16)]
     dma = pltpu.SemaphoreType.DMA
     scratch += [
-        dma((6,)),
+        dma((8,)),
         dma((2, groups)), dma((2, groups)),
-        dma((planes,)), dma((planes,)),
+        dma((planes, HALVES)), dma((planes, HALVES)),
         dma((planes, around)), dma((planes, around)),
         dma((number, 2, slots, around)), dma((number, 2, slots, around)),
         dma((2, planes)), dma((2, planes)),
         dma((CHUNKS, groups)), dma((CHUNKS, groups)),
         dma((CHUNKS, count)), dma((CHUNKS, count)),
     ]
-    return pl.pallas_call(
+    terms = pl.pallas_call(
         body,
-        out_shape=jax.ShapeDtypeStruct((own_tokens, width), f32),
-        in_specs=[smem] * 3 + [vmem] * 2 + [hbm] * 6,
+        out_shape=jax.ShapeDtypeStruct((CHUNKS, count, own_tokens, cut), bf16),
+        in_specs=[smem] * 3 + [hbm] * 8,
         out_specs=vmem,
         scratch_shapes=scratch,
         compiler_params=pltpu.CompilerParams(
@@ -873,9 +876,11 @@
         ),
         name="fused",
     )(
-        context_length, slot_sequence, slot_slab, q_compressed, draft_kv,
-        w_q_nope, w_q_rope, w_uk, w_uv, w_o, keys_hbm,
-    )
+        context_length, jnp.swapaxes(slot_sequence, 1, 2), jnp.swapaxes(slot_slab, 1, 2),
+        q_compressed, draft_kv, w_q_nope, w_q_rope, w_uk, w_uv, w_o, keys_hbm,
+    )
+    summed = jnp.sum(terms.astype(f32), axis=1)
+    return jnp.swapaxes(summed, 0, 1).reshape(own_tokens, width)
 
 
 def shards(
@@ -892,8 +897,9 @@
         w_uk.shape[0] % groups == 0
         and heads * DRAFT % 16 == 0
         and count % 2 == 0
-        and count // 2 in PHASES
+        and count // 2 in PLANES
         and q_compressed.shape[0] % count == 0
+        and groups * q_compressed.shape[0] // DRAFT % HALVES == 0
         and w_o.shape[1] % (128 * CHUNKS) == 0
     )
     if not fits:

time: 82.6 us -> 73.1 us (0.88)
  Pallas kernels: 78.1 us -> 71.1 us
  local copies, waits for them, and re-layouts: 4.12 us -> 0.64 us
  other arithmetic: 0 us -> 1.19 us
    pallas_call x1, Pallas kernels: 78.1 us -> 71.1 us  [fused(): pl.pallas_call(body, out_shape=jax.ShapeDtypeStruct((CHUNKS, count, own_t...]
    unnamed x3 -> x1, local copies, waits for them, and re-layouts: 4.12 us -> 0.64 us
    reduce_sum x0 -> x1, other arithmetic: none -> 1.19 us  [fused(): summed = jnp.sum(terms.astype(f32), axis=1)]
where the time goes in v2:
time: 73.1 us; the launch traced here: 72.9 us
  Pallas kernels  71.1 us (97%)
  other arithmetic  1.19 us (2%)
    pallas_call x1, Pallas kernels, fused(): pl.pallas_call(body, out_shape=jax.ShapeDtypeStruct((CHUNKS, count, own_t...  71.1 us

profile of v2, /device:TPU:0, one launch (start us, length us, event | category | flops | bytes accessed | tf_op | source)
XLA Modules:
  0.0 72.9 jit_solution(16919463366878101362)
XLA Ops:
  0.0 71.1 %fused.1 = bf16[4,8,1,1792]{3,2,1,0:T(2,128)(2,1)} custom-call(s32[8]{0:T(128)} %lengths.1, s32[4,2,8]{2,1,0:T(2,128)} %bitcast.10, s32[4,2,8]{2,1,0:T(2,128)} %bitcast.11, bf16[8,1536]{1,0:T(8,128)(2,1)} %qc.1, bf16[8,576]{1,0:T(8,128)(2,1)} %dkv.1, bf16[1536,2048]{1,0:T(8,128)(2,1)} %wqn_hbm.1, bf16[1536,1024]{1,0:T(8,128)(2,1)} %wqr_hbm.1, ...), custom_call_target="tpu_custom_call" | custom-call | tf_op jit(solution)/shard_map/fused/pallas_call | solution.py:868
  71.1 1.2 %convert_reduce_fusion = f32[4,1792]{1,0:T(4,128)S(1)} fusion(bf16[4,8,1,1792]{3,2,1,0:T(2,128)(2,1)} %fused.1), kind=kLoop, calls=%fused_computation | loop fusion | flops 107520 | bytes 143360 | tf_op jit(solution)/shard_map/reduce_sum | solution.py:882
  72.3 0.6 copy.12

commit v3 on v2

--- a/solution.py
+++ b/solution.py
@@ -391,7 +391,6 @@
     groups, count = lax.axis_size("group"), lax.axis_size("dev")
     planes = count // 2
     around = groups * 2
-    phases = tuple((s,) for s in range(planes))
     home_tokens, q_rank = q_compressed.shape
     tokens = groups * home_tokens
     seqs = tokens // DRAFT
@@ -402,8 +401,10 @@
     width = w_o.shape[1]
     nope_cols, rope_cols, out_rows = heads * NOPE, heads * ROPE, heads * VDIM
     cut = width // CHUNKS
+    own_tokens = home_tokens // count
     bf16, f32 = jnp.bfloat16, jnp.float32
-    number = len(phases)
+    tiles = LATENT // 128
+    all_tiles = slots * tiles + slots // 2
 
     def body(
         lengths, owners, slabs, qc, dkv, wqn_hbm, wqr_hbm, wuk_hbm, wuv_hbm, wo_hbm, cache, out,
@@ -411,9 +412,7 @@
     ):
         rest = list(rest)
         take = lambda n: [rest.pop(0) for _ in range(n)]
-        zb = take(planes)
-        staged = take(planes)
-        arrived, mixs, mixg, logs, logg = (take(number) for _ in range(5))
+        lat, rot, sided, staged, arrived, mixs, mixg, logs, logg = (take(planes) for _ in range(9))
         zms, zmg, zls, zlg = (take(planes) for _ in range(4))
         parts, partg, fin = take(3)
         (
@@ -465,32 +464,27 @@
         for step in range(1, around):
             greet(*plane_device(plane_peer(step)))
         for step in range(1, planes):
-            for core in range(2):
-                greet(g, lax.rem(z + step, planes) * 2 + core)
-        pl.semaphore_wait(barrier, around - 1 + 2 * (planes - 1))
-
-        def group_copies(step):
+            greet(g, lax.rem(z + step, planes) * 2 + c)
+        pl.semaphore_wait(barrier, around + planes - 2)
+
+        def group_copy(ref, which, step):
             to = lax.rem(g + step, groups)
-            return [
-                remote(qall.at[g], qall.at[g], g_send.at[0, step], g_recv.at[0, step], to, d),
-                remote(dall.at[g], dall.at[g], g_send.at[1, step], g_recv.at[1, step], to, d),
-            ]
-
-        for copy in early:
-            copy.wait()
+            return remote(
+                ref.at[g], ref.at[g], g_send.at[which, step], g_recv.at[which, step], to, d
+            )
+
+        for which, ref in enumerate((qall, dall)):
+            early[which].wait()
+            for step in reversed(range(1, groups)):
+                group_copy(ref, which, step).start()
         for step in range(1, groups):
-            for copy in group_copies(step):
-                copy.start()
-        for step in range(1, groups):
-            for copy in group_copies(step):
-                copy.wait()
+            group_copy(qall, 0, step).wait()
 
         def joined(ref):
             pieces = [ref[i].astype(f32) for i in range(groups)]
             return jnp.concatenate(pieces, axis=0).astype(bf16)
 
         q_tokens = joined(qall)
-        draft = joined(dall)
         for copy in loads[:3]:
             copy.wait()
         nope = jnp.dot(q_tokens, wqn[...], preferred_element_type=f32).astype(bf16)
@@ -509,118 +503,138 @@
         spot = spot + lax.div(row, unit) * DRAFT + lax.rem(row, DRAFT)
         order = jnp.where(col == spot, 1.0, 0.0).astype(bf16)
         queries = jnp.dot(order, stacked, preferred_element_type=f32).astype(bf16)
-        zb[0][...] = queries.reshape(seqs, unit, key_width)
-
-        def z_copy(s, half):
+        for i in range(tiles):
+            lat[0][:, i] = queries[:, i * 128 : (i + 1) * 128].reshape(seqs, unit, 128)
+        turned = queries[:, LATENT:].astype(f32)
+        for i in range(seqs // 2):
+            halves = [turned[(2 * i + j) * unit : (2 * i + j + 1) * unit] for j in range(2)]
+            rot[0][i] = jnp.concatenate(halves, axis=1).astype(bf16)
+
+        def z_copies(s, half):
             relay = s & 1 and s > 1
-            source, over = (zb[s ^ 1], 1) if relay else (zb[0], s)
-            span = pl.ds(half * seqs // HALVES, seqs // HALVES)
-            return remote(
-                source.at[span], zb[s].at[span], z_send.at[s, half], z_recv.at[s, half],
-                g, flip(z, over, planes) * 2 + c,
-            )
+            copies = []
+            for which, ref in enumerate((lat, rot)):
+                source, over = (ref[s ^ 1], 1) if relay else (ref[0], s)
+                size = seqs // HALVES // (1 + which)
+                span = pl.ds(half * size, size)
+                copies.append(
+                    remote(
+                        source.at[span], ref[s].at[span], z_send.at[which, s, half],
+                        z_recv.at[which, s, half], g, flip(z, over, planes) * 2 + c,
+                    )
+                )
+            return copies
 
         for half in range(HALVES):
             for s in reversed(range(1, planes)):
                 if not (s & 1 and s > 1):
-                    z_copy(s, half).start()
-
-        place = [(p, phases[p].index(s)) for s in range(planes) for p in range(number) if s in phases[p]]
-
-        def p_copy(s, to):
-            p, at = place[s]
+                    for copy in z_copies(s, half):
+                        copy.start()
+
+        def p_copy(s, to, source):
             return remote(
-                staged[s].at[to], arrived[p].at[me, :, at], p_send.at[s, to], p_recv.at[s, me],
+                staged[s].at[to], arrived[s].at[source], p_send.at[s, to], p_recv.at[s, source],
                 *plane_device(to),
             )
 
-        def p_arrival(s, source):
-            p, at = place[s]
-            return remote(
-                staged[s].at[source], arrived[p].at[source, :, at], p_send.at[s, source],
-                p_recv.at[s, source], *plane_device(source),
-            )
+        lane_of = lax.broadcasted_iota(jnp.int32, (unit, 128), 1)
+
+        def spread(s):
+            for i in range(seqs // 2):
+                tile = rot[s][i].astype(f32)
+                swapped = jnp.concatenate([tile[:, ROPE:], tile[:, :ROPE]], axis=1).astype(bf16)
+                for side in range(2):
+                    sided[s][side, 2 * i + side] = rot[s][i]
+                    sided[s][side, 2 * i + 1 - side] = swapped
+
+        def pack(dest, at, s, chosen):
+            for k in range(slots):
+                dest[at, k * tiles : (k + 1) * tiles] = lat[s][chosen[k]]
+            for k in range(0, slots, 2):
+                sides = [sided[s][side, chosen[k + side]].astype(f32) for side in range(2)]
+                both = jnp.where(lane_of < ROPE, sides[0], sides[1])
+                dest[at, slots * tiles + k // 2] = both.astype(bf16)
 
         def dispatch(s):
-            p, at = place[s]
-            if s > 0:
+            if s > 0 and (s % 2 == 1 or s + 1 == planes):
                 for half in range(HALVES):
-                    z_copy(s, half).wait_recv()
-                    if s % 2 == 0 and s + 1 < planes:
-                        z_copy(s + 1, half).start()
-
-            def fill(step, carry):
+                    for copy in z_copies(s, half):
+                        copy.wait_recv()
+
+            spread(s)
+            for step in range(1, around):
                 to = plane_peer(step)
                 to_g, to_d = plane_device(to)
-                for k in range(slots):
-                    staged[s][to, k] = zb[s][jnp.maximum(owners[to_g, k, to_d], 0)]
+                chosen = [jnp.maximum(owners[to_g, k, to_d], 0) for k in range(slots)]
+                pack(staged[s], to, s, chosen)
+
+            def send(step, carry):
+                p_copy(s, plane_peer(step), me).start()
                 return carry
 
-            def send(step, carry):
-                p_copy(s, plane_peer(step)).start()
-                return carry
-
-            lax.fori_loop(1, around, fill, 0)
             lax.fori_loop(1, around, send, 0)
-            for k in range(slots):
-                arrived[p][me, k, at] = zb[s][jnp.maximum(owners[g, k, d], 0)]
-
-        def b_copies(p, k, to, source):
+            pack(arrived[s], me, s, [jnp.maximum(owners[g, k, d], 0) for k in range(slots)])
+
+        def b_copies(p, to, source):
             return [
                 remote(
-                    mixs[p].at[k, to], mixg[p].at[source, k], b_send.at[p, 0, k, to],
-                    b_recv.at[p, 0, k, source], *plane_device(to),
-                ),
-                remote(
-                    logs[p].at[k, to], logg[p].at[source, k], b_send.at[p, 1, k, to],
-                    b_recv.at[p, 1, k, source], *plane_device(to),
-                ),
+                    stage.at[to], target.at[source], b_send.at[p, which, to],
+                    b_recv.at[p, which, source], *plane_device(to),
+                )
+                for which, (stage, target) in enumerate(((mixs[p], mixg[p]), (logs[p], logg[p])))
             ]
 
         def await_rows(p):
-            for s in phases[p]:
-
-                def one(step, carry):
-                    p_arrival(s, plane_peer(step)).wait_recv()
-                    return carry
-
-                lax.fori_loop(1, around, one, 0)
-
-        def attend(p, k):
-            some = len(phases[p])
-            per = some * unit
-            total_rows = around * per
-            owner = owners[g, k, d]
-            left = lengths[jnp.maximum(owner, 0)] - slabs[g, k, d] * slab_length
-            limit = jnp.where(owner >= 0, left, 0)
-            block = arrived[p][:, k].reshape(total_rows, key_width)
-            scores = lax.dot_general(
-                block, keys[k], (((1,), (0,)), ((), ())), preferred_element_type=f32
-            )
+            def one(step, carry):
+                source = plane_peer(step)
+                p_copy(p, source, source).wait_recv()
+                return carry
+
+            lax.fori_loop(1, around, one, 0)
+
+        def attend(p, chosen):
+            total_rows = around * unit
             position = lax.broadcasted_iota(jnp.int32, (1, slab_length), 1)
-            is_valid = position < limit
-            masked = jnp.where(is_valid, scores, EMPTY)
-            peak = jnp.max(masked, axis=1, keepdims=True)
-            weights = jnp.where(is_valid, jnp.exp(masked - peak), 0.0)
-            total = jnp.maximum(jnp.sum(weights, axis=1, keepdims=True), 1.0)
-            mixture = lax.dot_general(
-                weights.astype(bf16), keys[k, :LATENT], (((1,), (1,)), ((), ())),
-                preferred_element_type=f32,
-            )
-            mixs[p][k] = (mixture / total).astype(bf16).reshape(around, some, unit, LATENT)
-            log = jnp.broadcast_to(peak + jnp.log(total), (total_rows, 128))
-            log = jnp.transpose(log)[:1]
-            for j in range(around):
-                logs[p][k, j, :, :per] = log[:, j * per : (j + 1) * per]
-
+            scored = []
+            for k in chosen:
+                owner = owners[g, k, d]
+                left = lengths[jnp.maximum(owner, 0)] - slabs[g, k, d] * slab_length
+                cells = [arrived[p][:, k * tiles + i] for i in range(tiles)]
+                cells = [cell.reshape(total_rows, 128) for cell in cells]
+                turned = arrived[p][:, slots * tiles + k // 2].reshape(total_rows, 128)
+                side = k % 2 * ROPE
+                block = jnp.concatenate(cells + [turned[:, side : side + ROPE]], axis=1)
+                scores = lax.dot_general(
+                    block, keys[k], (((1,), (0,)), ((), ())), preferred_element_type=f32
+                )
+                scored.append((k, scores, position < jnp.where(owner >= 0, left, 0)))
+            weighed = []
+            for k, scores, is_valid in scored:
+                masked = jnp.where(is_valid, scores, EMPTY)
+                peak = jnp.max(masked, axis=1, keepdims=True)
+                weights = jnp.where(is_valid, jnp.exp(masked - peak), 0.0)
+                total = jnp.maximum(jnp.sum(weights, axis=1, keepdims=True), 1.0)
+                weighed.append((k, weights.astype(bf16), peak, total))
+            for k, weights, peak, total in weighed:
+                mixture = lax.dot_general(
+                    weights, keys[k, :LATENT], (((1,), (1,)), ((), ())),
+                    preferred_element_type=f32,
+                )
+                mixs[p][:, k] = (mixture / total).astype(bf16).reshape(around, unit, LATENT)
+                log = jnp.broadcast_to(peak + jnp.log(total), (total_rows, 128))
+                log = jnp.transpose(log)[:1]
+                for j in range(around):
+                    logs[p][j, k : k + 1, :unit] = log[:, j * unit : (j + 1) * unit]
+
+        def give_back(p):
             def send(step, carry):
-                for copy in b_copies(p, k, plane_peer(step), me):
+                for copy in b_copies(p, plane_peer(step), me):
                     copy.start()
                 return carry
 
             lax.fori_loop(1, around, send, 0)
-            mixg[p][me, k] = mixs[p][k, me]
-            logg[p][me, k] = logs[p][k, me]
+            mixg[p][me] = mixs[p][me]
+            logg[p][me] = logs[p][me]
 
         def split_dot(weights, block):
             high = weights.astype(bf16)
@@ -637,20 +651,18 @@
             ]
 
         def merge_plane(p):
-            some = len(phases[p])
-            per = some * unit
+            per = unit
             blocks = around * slots
 
             def one(step, carry):
                 source = plane_peer(step)
-                for k in range(slots):
-                    for copy in b_copies(p, k, source, source):
-                        copy.wait_recv()
+                for copy in b_copies(p, source, source):
+                    copy.wait_recv()
                 return carry
 
             lax.fori_loop(1, around, one, 0)
             wide = blocks * per
-            cells = [logg[p][j, k, :, :per] for j in range(around) for k in range(slots)]
+            cells = [logg[p][j, k : k + 1, :per] for j in range(around) for k in range(slots)]
             log = jnp.concatenate(cells, axis=1)
             lane = lax.broadcasted_iota(jnp.int32, (1, wide), 1)
             owner = jnp.full((1, wide), -1, jnp.int32)
@@ -659,29 +671,33 @@
                     here = owners[j // 2, k, z * 2 + j % 2]
                     owner = jnp.where(lax.div(lane, per) == j * slots + k, here, owner)
             tag = owner * per + lax.rem(lane, per)
-            height = some * rows
-            line = lax.broadcasted_iota(jnp.int32, (height, 1), 0)
-            inner = lax.div(line, rows) * unit + lax.rem(line, unit)
-            mark = lax.rem(lax.div(line, unit), seqs) * per + inner
-            match = tag == mark
+            line = lax.broadcasted_iota(jnp.int32, (rows, 1), 0)
+            match = tag == line
             picked = jnp.where(match, log, EMPTY)
             top = jnp.max(picked, axis=1, keepdims=True)
             weights = jnp.where(match, jnp.exp(picked - top), 0.0)
             total = jnp.maximum(jnp.sum(weights, axis=1, keepdims=True), 1.0)
             block = mixg[p][...].reshape(wide, LATENT)
             mixed = (split_dot(weights, block) / total).astype(bf16)
-            logged = jnp.broadcast_to(top + jnp.log(total), (height, 128))
-            logged = jnp.transpose(logged)[:1]
-            for at, s in enumerate(phases[p]):
-                mix_to, log_to = (zms[s], zls[s]) if s > 0 else (zmg[s], zlg[s])
-                mix_to[...] = mixed[at * rows : (at + 1) * rows]
-                log_to[...] = logged[:, at * rows : (at + 1) * rows]
-            for s in phases[p]:
-                if s > 0:
-                    for copy in y_copy(s):
-                        copy.start()
+            logged = jnp.broadcast_to(top + jnp.log(total), (rows, 128))
+            mix_to, log_to = (zms[p], zls[p]) if p > 0 else (zmg[p], zlg[p])
+            mix_to[...] = mixed
+            log_to[...] = jnp.transpose(logged)[:1]
+            if p > 0:
+                for copy in y_copy(p):
+                    copy.start()
+
+        def relay(half):
+            for s in range(2, planes - 1, 2):
+                for copy in z_copies(s, half):
+                    copy.wait_recv()
+                for copy in z_copies(s + 1, half):
+                    copy.start()
 
         dispatch(0)
+        for step in range(1, groups):
+            group_copy(dall, 1, step).wait()
+        draft = joined(dall)
         scores = lax.dot_general(
             queries, draft, (((1,), (1,)), ((), ())), preferred_element_type=f32
         )
@@ -698,24 +714,36 @@
         draft_mix = draft_mix / draft_total
         draft_log = draft_peak + jnp.log(draft_total)
 
-        def attend_both(p):
-            def one(k, carry):
-                attend(p, k)
-                return carry
-
+        every = range(slots)
+
+        def attend_all(p):
             await_rows(p)
-            lax.fori_loop(0, slots, one, 0)
+            attend(p, every)
+            give_back(p)
 
         loads[3].wait()
-        attend_both(0)
-        for s in range(1, planes):
-            dispatch(s)
-        merge_plane(0)
-        for p in range(1, number):
-            attend_both(p)
-            if p > 1:
-                merge_plane(p - 1)
-        merge_plane(number - 1)
+        await_rows(0)
+        attend(0, every)
+        for half in range(HALVES):
+            relay(half)
+        if planes == 4:
+            dispatch(2)
+            dispatch(3)
+            attend_all(2)
+            dispatch(1)
+            attend_all(3)
+            merge_plane(2)
+            attend_all(1)
+            give_back(0)
+            merge_plane(3)
+            merge_plane(1)
+            merge_plane(0)
+        else:
+            give_back(0)
+            dispatch(1)
+            merge_plane(0)
+            attend_all(1)
+            merge_plane(1)
 
         for s in range(1, planes):
             for copy in y_copy(s):
@@ -735,7 +763,11 @@
         attended = (summed / total).astype(bf16)
         row = lax.broadcasted_iota(jnp.int32, (rows, rows), 0)
         col = lax.broadcasted_iota(jnp.int32, (rows, rows), 1)
-        token = lax.rem(row, tokens)
+        rank = lax.rem(row, tokens)
+        share = planes * own_tokens
+        line = lax.rem(lax.div(rank, own_tokens), planes) * 2 + lax.rem(lax.div(rank, share), 2)
+        token = lax.div(rank, 2 * share) * home_tokens + line * own_tokens
+        token = token + lax.rem(rank, own_tokens)
         spot = lax.div(token, DRAFT) * unit + lax.div(row, tokens) * DRAFT + lax.rem(token, DRAFT)
         order = jnp.where(col == spot, 1.0, 0.0).astype(bf16)
         attended = jnp.dot(order, attended, preferred_element_type=f32).astype(bf16)
@@ -747,82 +779,83 @@
         ]
         values = jnp.concatenate(values, axis=1).astype(bf16)
 
-        def r_copy(n, step):
-            to = lax.rem(g + step, groups)
+        def r_copy(n, to, source):
             return remote(
-                parts.at[n, to], partg.at[n, g], r_send.at[n, step], r_recv.at[n, step], to, d
+                parts.at[n, to], partg.at[n, source], r_send.at[n, to], r_recv.at[n, source],
+                *plane_device(to),
             )
 
         def project(n, carry):
             span = pl.ds(pl.multiple_of(n * cut, 128), cut)
             part = jnp.dot(values, wo[:, span], preferred_element_type=f32)
-            for i in range(groups):
-                parts[n, i] = part[i * home_tokens : (i + 1) * home_tokens].astype(bf16)
-            for step in range(1, groups):
-                r_copy(n, step).start()
-            partg[n, g] = parts[n, g]
+            for j in range(around):
+                parts[n, j] = part[j * share : (j + 1) * share].astype(bf16)
+
+            def send(step, carry):
+                r_copy(n, plane_peer(step), me).start()
+                return carry
+
+            lax.fori_loop(1, around, send, 0)
+            partg[n, me] = parts[n, me]
             return carry
 
         lax.fori_loop(0, CHUNKS, project, 0)
+
+        def lane_span(n):
+            return pl.ds(pl.multiple_of(n * cut, 128), cut)
 
         def f_copy(n, to, source):
             return remote(
-                fin.at[n, to], out.at[n, source], f_send.at[n, to], f_recv.at[n, source], g, to
-            )
-
-        own_tokens = home_tokens // count
+                fin.at[n, to], out.at[source, :, lane_span(n)], f_send.at[n, to], f_recv.at[n, source],
+                g, to * 2 + c,
+            )
 
         def gather(n, carry):
-            for step in range(1, groups):
-                r_copy(n, step).wait_recv()
+            def arrive(step, carry):
+                source = plane_peer(step)
+                r_copy(n, source, source).wait_recv()
+                return carry
+
+            lax.fori_loop(1, around, arrive, 0)
             summed = partg[n, 0].astype(f32)
-            for i in range(1, groups):
-                summed = summed + partg[n, i].astype(f32)
-            for t in range(count):
+            for j in range(1, around):
+                summed = summed + partg[n, j].astype(f32)
+            for t in range(planes):
                 fin[n, t] = summed[t * own_tokens : (t + 1) * own_tokens].astype(bf16)
-
-            def send(step, carry):
-                f_copy(n, lax.rem(d + step, count), d).start()
-                return carry
-
-            lax.fori_loop(1, count, send, 0)
-            out[n, d] = fin[n, d]
+            for step in range(1, planes):
+                f_copy(n, lax.rem(z + step, planes), z).start()
+            out[z, :, lane_span(n)] = fin[n, z]
             return carry
 
         lax.fori_loop(0, CHUNKS, gather, 0)
 
         for n in range(CHUNKS):
-
-            def one(step, carry):
-                source = lax.rem(d + step, count)
+            for step in range(1, planes):
+                source = lax.rem(z + step, planes)
                 f_copy(n, source, source).wait_recv()
-                return carry
-
-            lax.fori_loop(1, count, one, 0)
 
         for s in range(1, planes):
             for half in range(HALVES):
-                z_copy(s, half).wait_send()
+                for copy in z_copies(s, half):
+                    copy.wait_send()
             for copy in y_copy(s):
                 copy.wait_send()
 
         def finish(step, carry):
             to = plane_peer(step)
             for s in range(planes):
-                p_copy(s, to).wait_send()
-            for p in range(number):
-                for k in range(slots):
-                    for copy in b_copies(p, k, to, me):
-                        copy.wait_send()
+                p_copy(s, to, me).wait_send()
+                for copy in b_copies(s, to, me):
+                    copy.wait_send()
             return carry
 
         lax.fori_loop(1, around, finish, 0)
 
         def finish_chunk(n, carry):
-            for step in range(1, groups):
-                r_copy(n, step).wait_send()
-            for step in range(1, count):
-                f_copy(n, lax.rem(d + step, count), d).wait_send()
+            for step in range(1, around):
+                r_copy(n, plane_peer(step), me).wait_send()
+            for step in range(1, planes):
+                f_copy(n, lax.rem(z + step, planes), z).wait_send()
             return carry
 
         lax.fori_loop(0, CHUNKS, finish_chunk, 0)
@@ -830,7 +863,6 @@
     smem = pl.BlockSpec(memory_space=pltpu.SMEM)
     vmem = pl.BlockSpec(memory_space=pltpu.VMEM)
     hbm = pl.BlockSpec(memory_space=pl.ANY)
-    own_tokens = home_tokens // count
     scratch = [
         pltpu.VMEM((groups, home_tokens, q_rank), bf16),
         pltpu.VMEM((groups, home_tokens, key_width), bf16),
@@ -841,33 +873,36 @@
         pltpu.VMEM((out_rows, width), bf16),
         pltpu.VMEM((slots, key_width, slab_length), bf16),
     ]
-    scratch += [pltpu.VMEM((seqs, unit, key_width), bf16) for _ in range(planes)]
-    scratch += [pltpu.VMEM((around, slots, unit, key_width), bf16) for _ in range(planes)]
-    sizes = [len(phase) for phase in phases]
-    scratch += [pltpu.VMEM((around, slots, n, unit, key_width), bf16) for n in sizes]
-    scratch += [pltpu.VMEM((slots, around, n, unit, LATENT), bf16) for n in sizes]
-    scratch += [pltpu.VMEM((around, slots, n, unit, LATENT), bf16) for n in sizes]
-    lanes = [-(-n * unit // 128) * 128 for n in sizes]
-    scratch += [pltpu.VMEM((slots, around, 1, n), f32) for n in lanes]
-    scratch += [pltpu.VMEM((around, slots, 1, n), f32) for n in lanes]
+    shapes = [
+        ((seqs, tiles, unit, 128), bf16),
+        ((seqs // 2, unit, 128), bf16),
+        ((2, seqs, unit, 128), bf16),
+        ((around, all_tiles, unit, 128), bf16),
+        ((around, all_tiles, unit, 128), bf16),
+        ((around, slots, unit, LATENT), bf16),
+        ((around, slots, unit, LATENT), bf16),
+        ((around, slots, 128), f32),
+        ((around, slots, 128), f32),
+    ]
+    scratch += [pltpu.VMEM(*shape) for shape in shapes for _ in range(planes)]
     scratch += [pltpu.VMEM((rows, LATENT), bf16) for _ in range(2 * planes)]
     scratch += [pltpu.VMEM((1, rows), f32) for _ in range(2 * planes)]
-    scratch += [pltpu.VMEM((CHUNKS, groups, home_tokens, cut), bf16) for _ in range(2)]
-    scratch += [pltpu.VMEM((CHUNKS, count, own_tokens, cut), bf16)]
+    scratch += [pltpu.VMEM((CHUNKS, around, planes * own_tokens, cut), bf16) for _ in range(2)]
+    scratch += [pltpu.VMEM((CHUNKS, planes, own_tokens, cut), bf16)]
     dma = pltpu.SemaphoreType.DMA
     scratch += [
         dma((8,)),
         dma((2, groups)), dma((2, groups)),
-        dma((planes, HALVES)), dma((planes, HALVES)),
+        dma((2, planes, HALVES)), dma((2, planes, HALVES)),
         dma((planes, around)), dma((planes, around)),
-        dma((number, 2, slots, around)), dma((number, 2, slots, around)),
+        dma((planes, 2, around)), dma((planes, 2, around)),
         dma((2, planes)), dma((2, planes)),
-        dma((CHUNKS, groups)), dma((CHUNKS, groups)),
-        dma((CHUNKS, count)), dma((CHUNKS, count)),
+        dma((CHUNKS, around)), dma((CHUNKS, around)),
+        dma((CHUNKS, planes)), dma((CHUNKS, planes)),
     ]
     terms = pl.pallas_call(
         body,
-        out_shape=jax.ShapeDtypeStruct((CHUNKS, count, own_tokens, cut), bf16),
+        out_shape=jax.ShapeDtypeStruct((planes, own_tokens, width), bf16),
         in_specs=[smem] * 3 + [hbm] * 8,
         out_specs=vmem,
         scratch_shapes=scratch,
@@ -879,8 +914,7 @@
         context_length, jnp.swapaxes(slot_sequence, 1, 2), jnp.swapaxes(slot_slab, 1, 2),
         q_compressed, draft_kv, w_q_nope, w_q_rope, w_uk, w_uv, w_o, keys_hbm,
     )
-    summed = jnp.sum(terms.astype(f32), axis=1)
-    return jnp.swapaxes(summed, 0, 1).reshape(own_tokens, width)
+    return jnp.sum(terms.astype(f32), axis=0)
 
 
 def shards(
@@ -895,11 +929,12 @@
     heads = w_uk.shape[0] // groups
     fits = (
         w_uk.shape[0] % groups == 0
-        and heads * DRAFT % 16 == 0
         and count % 2 == 0
         and count // 2 in PLANES
         and q_compressed.shape[0] % count == 0
-        and groups * q_compressed.shape[0] // DRAFT % HALVES == 0
+        and groups * q_compressed.shape[0] // DRAFT % (2 * HALVES) == 0
+        and kv_cache.shape[2] % 2 == 0
+        and heads * DRAFT == 16
         and w_o.shape[1] % (128 * CHUNKS) == 0
     )
     if not fits:

time: 73.1 us -> 65.2 us (0.89)
  Pallas kernels: 71.1 us -> 63.4 us
    pallas_call x1, Pallas kernels: 71.1 us -> 63.4 us  [fused(): pl.pallas_call(body, out_shape=jax.ShapeDtypeStruct((planes, own_tokens,...]
where the time goes in v3:
time: 65.2 us; the launch traced here: 65 us
  Pallas kernels  63.4 us (97%)
  other arithmetic  1.65 us (3%)
    pallas_call x1, Pallas kernels, fused(): pl.pallas_call(body, out_shape=jax.ShapeDtypeStruct((planes, own_tokens,...  63.4 us
    reduce_sum x1, other arithmetic, fused(): return jnp.sum(terms.astype(f32), axis=0)  1.65 us

profile of v3, /device:TPU:0, one launch (start us, length us, event | category | flops | bytes accessed | tf_op | source)
XLA Modules:
  0.0 65.0 jit_solution(2968152923344322228)
XLA Ops:
  0.0 63.4 %fused.1 = bf16[4,1,7168]{2,1,0:T(2,128)(2,1)} custom-call(s32[8]{0:T(128)} %lengths.1, s32[4,2,8]{2,1,0:T(2,128)} %bitcast.7, s32[4,2,8]{2,1,0:T(2,128)} %bitcast.8, bf16[8,1536]{1,0:T(8,128)(2,1)} %qc.1, bf16[8,576]{1,0:T(8,128)(2,1)} %dkv.1, bf16[1536,2048]{1,0:T(8,128)(2,1)} %wqn_hbm.1, bf16[1536,1024]{1,0:T(8,128)(2,1)} %wqr_hbm.1, ...), custom_call_target="tpu_custom_call" | custom-call | tf_op jit(solution)/shard_map/fused/pallas_call | solution.py:903
  63.4 1.7 %convert_reduce_fusion = f32[7168]{0:T(1024)} fusion(bf16[4,1,7168]{2,1,0:T(2,128)(2,1)} %fused.1), kind=kLoop, calls=%fused_computation | loop fusion | flops 50176 | bytes 86016 | tf_op jit(solution)/shard_map/reduce_sum | solution.py:917

commit v4 on v3

--- a/solution.py
+++ b/solution.py
@@ -373,6 +373,7 @@
 PLANES = (2, 4)
 HALVES = 2
 CHUNKS = 4
+VMEM_LIMIT = 56 * 1024 * 1024
 
 
 def flip(value, mask, extent):
@@ -470,15 +471,20 @@
         def group_copy(ref, which, step):
             to = lax.rem(g + step, groups)
             return remote(
-                ref.at[g], ref.at[g], g_send.at[which, step], g_recv.at[which, step], to, d
-            )
+                ref.at[g], ref.at[g], g_send.at[which], g_recv.at[which], to, d
+            )
+
+        def group_wait(ref, which):
+            most = ref.at[pl.ds(0, groups - 1)]
+            remote(
+                most, most, g_send.at[which], g_recv.at[which], lax.rem(g + 1, groups), d
+            ).wait()
 
         for which, ref in enumerate((qall, dall)):
             early[which].wait()
             for step in reversed(range(1, groups)):
                 group_copy(ref, which, step).start()
-        for step in range(1, groups):
-            group_copy(qall, 0, step).wait()
+        group_wait(qall, 0)
 
         def joined(ref):
             pieces = [ref[i].astype(f32) for i in range(groups)]
@@ -533,9 +539,26 @@
 
         def p_copy(s, to, source):
             return remote(
-                staged[s].at[to], arrived[s].at[source], p_send.at[s, to], p_recv.at[s, source],
+                staged[s].at[to], arrived[s].at[source], p_send.at[s], p_recv.at[s],
                 *plane_device(to),
             )
+
+        most = pl.ds(0, around - 1)
+        next_device = plane_device(plane_peer(1))
+
+        def p_whole(s):
+            return remote(
+                staged[s].at[most], arrived[s].at[most], p_send.at[s], p_recv.at[s], *next_device
+            )
+
+        def b_whole(p):
+            return [
+                remote(
+                    stage.at[most], target.at[most], b_send.at[p, which], b_recv.at[p, which],
+                    *next_device,
+                )
+                for which, (stage, target) in enumerate(((mixs[p], mixg[p]), (logs[p], logg[p])))
+            ]
 
         lane_of = lax.broadcasted_iota(jnp.int32, (unit, 128), 1)
 
@@ -578,19 +601,14 @@
         def b_copies(p, to, source):
             return [
                 remote(
-                    stage.at[to], target.at[source], b_send.at[p, which, to],
-                    b_recv.at[p, which, source], *plane_device(to),
+                    stage.at[to], target.at[source], b_send.at[p, which],
+                    b_recv.at[p, which], *plane_device(to),
                 )
                 for which, (stage, target) in enumerate(((mixs[p], mixg[p]), (logs[p], logg[p])))
             ]
 
         def await_rows(p):
-            def one(step, carry):
-                source = plane_peer(step)
-                p_copy(p, source, source).wait_recv()
-                return carry
-
-            lax.fori_loop(1, around, one, 0)
+            p_whole(p).wait_recv()
 
         def attend(p, chosen):
             total_rows = around * unit
@@ -650,17 +668,17 @@
                 remote(zls[s], zlg[s], y_send.at[1, s], y_recv.at[1, s], g, to),
             ]
 
+        def column_of(s):
+            lane = lax.broadcasted_iota(jnp.int32, (rows, rows), 1)
+            line = lax.broadcasted_iota(jnp.int32, (rows, rows), 0)
+            return jnp.max(jnp.where(lane == line, zlg[s][...], EMPTY), axis=1, keepdims=True)
+
         def merge_plane(p):
             per = unit
             blocks = around * slots
 
-            def one(step, carry):
-                source = plane_peer(step)
-                for copy in b_copies(p, source, source):
-                    copy.wait_recv()
-                return carry
-
-            lax.fori_loop(1, around, one, 0)
+            for copy in b_whole(p):
+                copy.wait_recv()
             wide = blocks * per
             cells = [logg[p][j, k : k + 1, :per] for j in range(around) for k in range(slots)]
             log = jnp.concatenate(cells, axis=1)
@@ -695,8 +713,7 @@
                     copy.start()
 
         dispatch(0)
-        for step in range(1, groups):
-            group_copy(dall, 1, step).wait()
+        group_wait(dall, 1)
         draft = joined(dall)
         scores = lax.dot_general(
             queries, draft, (((1,), (1,)), ((), ())), preferred_element_type=f32
@@ -716,9 +733,12 @@
 
         every = range(slots)
 
-        def attend_all(p):
+        def attend_only(p):
             await_rows(p)
             attend(p, every)
+
+        def attend_all(p):
+            attend_only(p)
             give_back(p)
 
         loads[3].wait()
@@ -728,15 +748,15 @@
             relay(half)
         if planes == 4:
             dispatch(2)
+            dispatch(1)
             dispatch(3)
             attend_all(2)
-            dispatch(1)
+            attend_all(1)
             attend_all(3)
+            give_back(0)
             merge_plane(2)
-            attend_all(1)
-            give_back(0)
+            merge_plane(1)
             merge_plane(3)
-            merge_plane(1)
             merge_plane(0)
         else:
             give_back(0)
@@ -745,21 +765,29 @@
             attend_all(1)
             merge_plane(1)
 
+        for s in range(planes):
+            p_whole(s).wait_send()
+            for copy in b_whole(s):
+                copy.wait_send()
         for s in range(1, planes):
+            for half in range(HALVES):
+                for copy in z_copies(s, half):
+                    copy.wait_send()
+
+        all_planes = range(planes)
+        for s in all_planes[1:]:
             for copy in y_copy(s):
                 copy.wait_recv()
-        wide = planes * rows
-        log = jnp.concatenate([zlg[s][...] for s in range(planes)], axis=1)
-        lane = lax.broadcasted_iota(jnp.int32, (1, wide), 1)
-        line = lax.broadcasted_iota(jnp.int32, (rows, 1), 0)
-        match = lax.rem(lane, rows) == line
-        picked = jnp.where(match, log, EMPTY)
-        top = jnp.maximum(jnp.max(picked, axis=1, keepdims=True), draft_log)
-        weights = jnp.where(match, jnp.exp(picked - top), 0.0)
-        own = jnp.exp(draft_log - top)
-        total = jnp.sum(weights, axis=1, keepdims=True) + own
-        block = jnp.concatenate([zmg[s][...] for s in range(planes)], axis=0)
-        summed = split_dot(weights, block) + own * draft_mix
+        tops = [column_of(s) for s in all_planes]
+        top = draft_log
+        for log in tops:
+            top = jnp.maximum(top, log)
+        total = jnp.exp(draft_log - top)
+        summed = total * draft_mix
+        for s in all_planes:
+            weight = jnp.exp(tops[s] - top)
+            total = total + weight
+            summed = summed + weight * zmg[s][...].astype(f32)
         attended = (summed / total).astype(bf16)
         row = lax.broadcasted_iota(jnp.int32, (rows, rows), 0)
         col = lax.broadcasted_iota(jnp.int32, (rows, rows), 1)
@@ -781,8 +809,13 @@
 
         def r_copy(n, to, source):
             return remote(
-                parts.at[n, to], partg.at[n, source], r_send.at[n, to], r_recv.at[n, source],
+                parts.at[n, to], partg.at[n, source], r_send.at[n], r_recv.at[n],
                 *plane_device(to),
+            )
+
+        def r_whole(n):
+            return remote(
+                parts.at[n, most], partg.at[n, most], r_send.at[n], r_recv.at[n], *next_device
             )
 
         def project(n, carry):
@@ -806,17 +839,19 @@
 
         def f_copy(n, to, source):
             return remote(
-                fin.at[n, to], out.at[source, :, lane_span(n)], f_send.at[n, to], f_recv.at[n, source],
+                fin.at[n, to], out.at[source, :, lane_span(n)], f_send.at[n], f_recv.at[n],
                 g, to * 2 + c,
             )
 
+        def f_whole(n):
+            rest = pl.ds(0, planes - 1)
+            return remote(
+                fin.at[n, rest], out.at[rest, :, lane_span(n)], f_send.at[n], f_recv.at[n],
+                g, lax.rem(z + 1, planes) * 2 + c,
+            )
+
         def gather(n, carry):
-            def arrive(step, carry):
-                source = plane_peer(step)
-                r_copy(n, source, source).wait_recv()
-                return carry
-
-            lax.fori_loop(1, around, arrive, 0)
+            r_whole(n).wait_recv()
             summed = partg[n, 0].astype(f32)
             for j in range(1, around):
                 summed = summed + partg[n, j].astype(f32)
@@ -829,36 +864,14 @@
 
         lax.fori_loop(0, CHUNKS, gather, 0)
 
-        for n in range(CHUNKS):
-            for step in range(1, planes):
-                source = lax.rem(z + step, planes)
-                f_copy(n, source, source).wait_recv()
-
         for s in range(1, planes):
-            for half in range(HALVES):
-                for copy in z_copies(s, half):
-                    copy.wait_send()
             for copy in y_copy(s):
                 copy.wait_send()
-
-        def finish(step, carry):
-            to = plane_peer(step)
-            for s in range(planes):
-                p_copy(s, to, me).wait_send()
-                for copy in b_copies(s, to, me):
-                    copy.wait_send()
-            return carry
-
-        lax.fori_loop(1, around, finish, 0)
-
-        def finish_chunk(n, carry):
-            for step in range(1, around):
-                r_copy(n, plane_peer(step), me).wait_send()
-            for step in range(1, planes):
-                f_copy(n, lax.rem(z + step, planes), z).wait_send()
-            return carry
-
-        lax.fori_loop(0, CHUNKS, finish_chunk, 0)
+        for n in range(CHUNKS):
+            r_whole(n).wait_send()
+            f_whole(n).wait_send()
+        for n in range(CHUNKS):
+            f_whole(n).wait_recv()
 
     smem = pl.BlockSpec(memory_space=pltpu.SMEM)
     vmem = pl.BlockSpec(memory_space=pltpu.VMEM)
@@ -892,13 +905,13 @@
     dma = pltpu.SemaphoreType.DMA
     scratch += [
         dma((8,)),
-        dma((2, groups)), dma((2, groups)),
+        dma((2,)), dma((2,)),
         dma((2, planes, HALVES)), dma((2, planes, HALVES)),
-        dma((planes, around)), dma((planes, around)),
-        dma((planes, 2, around)), dma((planes, 2, around)),
+        dma((planes,)), dma((planes,)),
+        dma((planes, 2)), dma((planes, 2)),
         dma((2, planes)), dma((2, planes)),
-        dma((CHUNKS, around)), dma((CHUNKS, around)),
-        dma((CHUNKS, planes)), dma((CHUNKS, planes)),
+        dma((CHUNKS,)), dma((CHUNKS,)),
+        dma((CHUNKS,)), dma((CHUNKS,)),
     ]
     terms = pl.pallas_call(
         body,
@@ -907,7 +920,7 @@
         out_specs=vmem,
         scratch_shapes=scratch,
         compiler_params=pltpu.CompilerParams(
-            collective_id=0, has_side_effects=True, vmem_limit_bytes=56 * 1024 * 1024
+            collective_id=0, has_side_effects=True, vmem_limit_bytes=VMEM_LIMIT
         ),
         name="fused",
     )(

time: 65.2 us -> 60.9 us (0.934)
  Pallas kernels: 63.4 us -> 59.1 us
    pallas_call x1, Pallas kernels: 63.4 us -> 59.1 us  [fused(): pl.pallas_call(body, out_shape=jax.ShapeDtypeStruct((planes, own_tokens,...]
where the time goes in v4:
time: 60.9 us; the launch traced here: 60.7 us
  Pallas kernels  59.1 us (97%)
  other arithmetic  1.65 us (3%)
    pallas_call x1, Pallas kernels, fused(): pl.pallas_call(body, out_shape=jax.ShapeDtypeStruct((planes, own_tokens,...  59.1 us
    reduce_sum x1, other arithmetic, fused(): return jnp.sum(terms.astype(f32), axis=0)  1.65 us

profile of v4, /device:TPU:0, one launch (start us, length us, event | category | flops | bytes accessed | tf_op | source)
XLA Modules:
  0.0 60.7 jit_solution(3473094033044621491)
XLA Ops:
  0.0 59.1 %fused.1 = bf16[4,1,7168]{2,1,0:T(2,128)(2,1)} custom-call(s32[8]{0:T(128)} %lengths.1, s32[4,2,8]{2,1,0:T(2,128)} %bitcast.7, s32[4,2,8]{2,1,0:T(2,128)} %bitcast.8, bf16[8,1536]{1,0:T(8,128)(2,1)} %qc.1, bf16[8,576]{1,0:T(8,128)(2,1)} %dkv.1, bf16[1536,2048]{1,0:T(8,128)(2,1)} %wqn_hbm.1, bf16[1536,1024]{1,0:T(8,128)(2,1)} %wqr_hbm.1, ...), custom_call_target="tpu_custom_call" | custom-call | tf_op jit(solution)/shard_map/fused/pallas_call | solution.py:916
  59.1 1.7 %convert_reduce_fusion = f32[7168]{0:T(1024)} fusion(bf16[4,1,7168]{2,1,0:T(2,128)(2,1)} %fused.1), kind=kLoop, calls=%fused_computation | loop fusion | flops 50176 | bytes 86016 | tf_op jit(solution)/shard_map/reduce_sum | solution.py:930

commit v5 on v4

--- a/solution.py
+++ b/solution.py
@@ -415,10 +415,10 @@
         take = lambda n: [rest.pop(0) for _ in range(n)]
         lat, rot, sided, staged, arrived, mixs, mixg, logs, logg = (take(planes) for _ in range(9))
         zms, zmg, zls, zlg = (take(planes) for _ in range(4))
-        parts, partg, fin = take(3)
+        parts, pairg, sums, partg, fin = take(5)
         (
             local, g_send, g_recv, z_send, z_recv, p_send, p_recv, b_send, b_recv,
-            y_send, y_recv, r_send, r_recv, f_send, f_recv,
+            y_send, y_recv, e_send, e_recv, r_send, r_recv, f_send, f_recv,
         ) = rest
         g = lax.axis_index("group")
         d = lax.axis_index("dev")
@@ -436,6 +436,18 @@
 
         def plane_device(j):
             return lax.div(j, 2), z * 2 + lax.rem(j, 2)
+
+        barrier = pltpu.get_barrier_semaphore()
+
+        def greet(to_g, to_d):
+            pl.semaphore_signal(
+                barrier, inc=1, device_id=(to_g, to_d), device_id_type=pl.DeviceIdType.MESH
+            )
+
+        for step in range(1, around):
+            greet(*plane_device(plane_peer(step)))
+        for step in range(1, planes):
+            greet(g, lax.rem(z + step, planes) * 2 + c)
 
         columns = lambda size: pl.ds(pl.multiple_of(g * size, size), size)
         early = [
@@ -454,22 +466,10 @@
         ]
         for copy in loads:
             copy.start()
-
-        barrier = pltpu.get_barrier_semaphore()
-
-        def greet(to_g, to_d):
-            pl.semaphore_signal(
-                barrier, inc=1, device_id=(to_g, to_d), device_id_type=pl.DeviceIdType.MESH
-            )
-
-        for step in range(1, around):
-            greet(*plane_device(plane_peer(step)))
-        for step in range(1, planes):
-            greet(g, lax.rem(z + step, planes) * 2 + c)
         pl.semaphore_wait(barrier, around + planes - 2)
 
         def group_copy(ref, which, step):
-            to = lax.rem(g + step, groups)
+            to = flip(g, step, groups) if groups == 4 else lax.rem(g + step, groups)
             return remote(
                 ref.at[g], ref.at[g], g_send.at[which], g_recv.at[which], to, d
             )
@@ -673,24 +673,21 @@
             line = lax.broadcasted_iota(jnp.int32, (rows, rows), 0)
             return jnp.max(jnp.where(lane == line, zlg[s][...], EMPTY), axis=1, keepdims=True)
 
+        wide = around * slots * unit
+        lane = lax.broadcasted_iota(jnp.int32, (1, wide), 1)
+        owner = jnp.full((1, wide), -1, jnp.int32)
+        for j in range(around):
+            for k in range(slots):
+                here = owners[j // 2, k, z * 2 + j % 2]
+                owner = jnp.where(lax.div(lane, unit) == j * slots + k, here, owner)
+        tag = owner * unit + lax.rem(lane, unit)
+        match = tag == lax.broadcasted_iota(jnp.int32, (rows, 1), 0)
+
         def merge_plane(p):
-            per = unit
-            blocks = around * slots
-
             for copy in b_whole(p):
                 copy.wait_recv()
-            wide = blocks * per
-            cells = [logg[p][j, k : k + 1, :per] for j in range(around) for k in range(slots)]
+            cells = [logg[p][j, k : k + 1, :unit] for j in range(around) for k in range(slots)]
             log = jnp.concatenate(cells, axis=1)
-            lane = lax.broadcasted_iota(jnp.int32, (1, wide), 1)
-            owner = jnp.full((1, wide), -1, jnp.int32)
-            for j in range(around):
-                for k in range(slots):
-                    here = owners[j // 2, k, z * 2 + j % 2]
-                    owner = jnp.where(lax.div(lane, per) == j * slots + k, here, owner)
-            tag = owner * per + lax.rem(lane, per)
-            line = lax.broadcasted_iota(jnp.int32, (rows, 1), 0)
-            match = tag == line
             picked = jnp.where(match, log, EMPTY)
             top = jnp.max(picked, axis=1, keepdims=True)
             weights = jnp.where(match, jnp.exp(picked - top), 0.0)
@@ -774,27 +771,28 @@
                 for copy in z_copies(s, half):
                     copy.wait_send()
 
-        all_planes = range(planes)
-        for s in all_planes[1:]:
+        def join(merged, s):
+            top, total, summed = merged
+            log = column_of(s)
+            higher = jnp.maximum(top, log)
+            scale, weight = jnp.exp(top - higher), jnp.exp(log - higher)
+            block = zmg[s][...].astype(f32)
+            return higher, scale * total + weight, scale * summed + weight * block
+
+        merged = join((draft_log, jnp.ones_like(draft_log), draft_mix), 0)
+        for s in (1, 2, 3)[: planes - 1]:
             for copy in y_copy(s):
                 copy.wait_recv()
-        tops = [column_of(s) for s in all_planes]
-        top = draft_log
-        for log in tops:
-            top = jnp.maximum(top, log)
-        total = jnp.exp(draft_log - top)
-        summed = total * draft_mix
-        for s in all_planes:
-            weight = jnp.exp(tops[s] - top)
-            total = total + weight
-            summed = summed + weight * zmg[s][...].astype(f32)
+            merged = join(merged, s)
+        top, total, summed = merged
         attended = (summed / total).astype(bf16)
         row = lax.broadcasted_iota(jnp.int32, (rows, rows), 0)
         col = lax.broadcasted_iota(jnp.int32, (rows, rows), 1)
         rank = lax.rem(row, tokens)
         share = planes * own_tokens
-        line = lax.rem(lax.div(rank, own_tokens), planes) * 2 + lax.rem(lax.div(rank, share), 2)
-        token = lax.div(rank, 2 * share) * home_tokens + line * own_tokens
+        half = groups * share
+        line = lax.rem(lax.div(rank, own_tokens), planes) * 2 + lax.div(rank, half)
+        token = lax.rem(lax.div(rank, share), groups) * home_tokens + line * own_tokens
         token = token + lax.rem(rank, own_tokens)
         spot = lax.div(token, DRAFT) * unit + lax.div(row, tokens) * DRAFT + lax.rem(token, DRAFT)
         order = jnp.where(col == spot, 1.0, 0.0).astype(bf16)
@@ -807,32 +805,47 @@
         ]
         values = jnp.concatenate(values, axis=1).astype(bf16)
 
-        def r_copy(n, to, source):
+        def pair_copy(n):
             return remote(
-                parts.at[n, to], partg.at[n, source], r_send.at[n], r_recv.at[n],
-                *plane_device(to),
+                parts.at[n, 1 - c], pairg.at[n], e_send.at[n], e_recv.at[n], g, z * 2 + 1 - c
+            )
+
+        def r_copy(n, to):
+            return remote(
+                sums.at[n, to], partg.at[n, g], r_send.at[n], r_recv.at[n], to, d
             )
 
         def r_whole(n):
+            rest = pl.ds(0, groups - 1)
             return remote(
-                parts.at[n, most], partg.at[n, most], r_send.at[n], r_recv.at[n], *next_device
-            )
-
-        def project(n, carry):
+                sums.at[n, rest], partg.at[n, rest], r_send.at[n], r_recv.at[n],
+                lax.rem(g + 1, groups), d,
+            )
+
+        def project(n):
             span = pl.ds(pl.multiple_of(n * cut, 128), cut)
             part = jnp.dot(values, wo[:, span], preferred_element_type=f32)
-            for j in range(around):
-                parts[n, j] = part[j * share : (j + 1) * share].astype(bf16)
-
-            def send(step, carry):
-                r_copy(n, plane_peer(step), me).start()
-                return carry
-
-            lax.fori_loop(1, around, send, 0)
-            partg[n, me] = parts[n, me]
+            for i in range(2):
+                parts[n, i] = part[i * half : (i + 1) * half].astype(bf16)
+            pair_copy(n).start()
+
+        def pair_up(n):
+            pair_copy(n).wait_recv()
+            both = parts[n, c].astype(f32) + pairg[n].astype(f32)
+            for i in range(groups):
+                sums[n, i] = both[i * share : (i + 1) * share].astype(bf16)
+            for step in reversed(range(1, groups)):
+                r_copy(n, lax.rem(g + step, groups)).start()
+            partg[n, g] = sums[n, g]
+
+        def project_on(n, carry):
+            project(n)
+            pair_up(n - 1)
             return carry
 
-        lax.fori_loop(0, CHUNKS, project, 0)
+        project(0)
+        lax.fori_loop(1, CHUNKS, project_on, 0)
+        pair_up(CHUNKS - 1)
 
         def lane_span(n):
             return pl.ds(pl.multiple_of(n * cut, 128), cut)
@@ -853,7 +866,7 @@
         def gather(n, carry):
             r_whole(n).wait_recv()
             summed = partg[n, 0].astype(f32)
-            for j in range(1, around):
+            for j in range(1, groups):
                 summed = summed + partg[n, j].astype(f32)
             for t in range(planes):
                 fin[n, t] = summed[t * own_tokens : (t + 1) * own_tokens].astype(bf16)
@@ -868,6 +881,7 @@
             for copy in y_copy(s):
                 copy.wait_send()
         for n in range(CHUNKS):
+            pair_copy(n).wait_send()
             r_whole(n).wait_send()
             f_whole(n).wait_send()
         for n in range(CHUNKS):
@@ -900,7 +914,12 @@
     scratch += [pltpu.VMEM(*shape) for shape in shapes for _ in range(planes)]
     scratch += [pltpu.VMEM((rows, LATENT), bf16) for _ in range(2 * planes)]
     scratch += [pltpu.VMEM((1, rows), f32) for _ in range(2 * planes)]
-    scratch += [pltpu.VMEM((CHUNKS, around, planes * own_tokens, cut), bf16) for _ in range(2)]
+    scratch += [
+        pltpu.VMEM((CHUNKS, 2, groups * planes * own_tokens, cut), bf16),
+        pltpu.VMEM((CHUNKS, groups * planes * own_tokens, cut), bf16),
+        pltpu.VMEM((CHUNKS, groups, planes * own_tokens, cut), bf16),
+        pltpu.VMEM((CHUNKS, groups, planes * own_tokens, cut), bf16),
+    ]
     scratch += [pltpu.VMEM((CHUNKS, planes, own_tokens, cut), bf16)]
     dma = pltpu.SemaphoreType.DMA
     scratch += [
@@ -910,6 +929,7 @@
         dma((planes,)), dma((planes,)),
         dma((planes, 2)), dma((planes, 2)),
         dma((2, planes)), dma((2, planes)),
+        dma((CHUNKS,)), dma((CHUNKS,)),
         dma((CHUNKS,)), dma((CHUNKS,)),
         dma((CHUNKS,)), dma((CHUNKS,)),
     ]

time: 60.9 us -> 59.9 us (0.984)
  Pallas kernels: 59.1 us -> 58 us
    pallas_call x1, Pallas kernels: 59.1 us -> 58 us  [fused(): pl.pallas_call(body, out_shape=jax.ShapeDtypeStruct((planes, own_tokens,...]
where the time goes in v5:
time: 59.9 us; the launch traced here: 59.7 us
  Pallas kernels  58 us (97%)
  other arithmetic  1.65 us (3%)
    pallas_call x1, Pallas kernels, fused(): pl.pallas_call(body, out_shape=jax.ShapeDtypeStruct((planes, own_tokens,...  58 us
    reduce_sum x1, other arithmetic, fused(): return jnp.sum(terms.astype(f32), axis=0)  1.65 us

profile of v5, /device:TPU:0, one launch (start us, length us, event | category | flops | bytes accessed | tf_op | source)
XLA Modules:
  0.0 59.7 jit_solution(9393947080120340247)
XLA Ops:
  0.0 58.0 %fused.1 = bf16[4,1,7168]{2,1,0:T(2,128)(2,1)} custom-call(s32[8]{0:T(128)} %lengths.1, s32[4,2,8]{2,1,0:T(2,128)} %bitcast.7, s32[4,2,8]{2,1,0:T(2,128)} %bitcast.8, bf16[8,1536]{1,0:T(8,128)(2,1)} %qc.1, bf16[8,576]{1,0:T(8,128)(2,1)} %dkv.1, bf16[1536,2048]{1,0:T(8,128)(2,1)} %wqn_hbm.1, bf16[1536,1024]{1,0:T(8,128)(2,1)} %wqr_hbm.1, ...), custom_call_target="tpu_custom_call" | custom-call | tf_op jit(solution)/shard_map/fused/pallas_call | solution.py:936
  58.0 1.7 %convert_reduce_fusion = f32[7168]{0:T(1024)} fusion(bf16[4,1,7168]{2,1,0:T(2,128)(2,1)} %fused.1), kind=kLoop, calls=%fused_computation | loop fusion | flops 50176 | bytes 86016 | tf_op jit(solution)/shard_map/reduce_sum | solution.py:950
